TPU v7x, 32 devices: a whole 2x2x4 slice. The times are simulated.
32 devices in a mesh: gx: 4 (over y, x), gy: 8 (over z, core).
Axes of the slice: x: 2, y: 2, z: 4, core: 2. Of those that a mesh axis runs over, the one named last changes fastest.
Arguments:
- fields: float32 [6, 16, 128, 512], P(None, None, 'gy', 'gx'), may hold values from -4 to 4
- velocity: float32 [2, 16, 128, 512], P(None, None, 'gy', 'gx'), may hold values from -1 to 1
- coupling: float32 [6], replicated, may hold values from 0.5 to 4
- positions: float32 [3, 4, 8, 1024], P(None, 'gx', 'gy'), may hold values from 0 to 512, as said below
- log_radius: float32 [4, 8, 1024], P('gx', 'gy'), may hold values from -0.35 to 0.35
- growth: float32 [4, 8, 1024], P('gx', 'gy'), may hold values from -0.5 to 0.5
- rest_gap: float32 [4, 8, 1024], P('gx', 'gy'), may hold values from -0.15 to 0.15
- gas_pressure: float32 [4, 8, 1024], P('gx', 'gy'), may hold values from 0.7 to 1.4
- move_codes: int32 [4, 8, 1024], P('gx', 'gy'), may hold values from 0 to 9, as said below
- targets: int32 [4, 8, 1024], P('gx', 'gy'), may hold values from 0 to 1023, as said below
Outputs:
- new_fields: float32 [6, 16, 128, 512], P(None, None, 'gy', 'gx')
- new_bubbles: float32 [2, 4, 8, 1024], P(None, 'gx', 'gy')
Inputs may be any that keep to these rules, and one draw needn't show every extreme that they name: `move_codes`: code 3 (a + 1) + (b + 1) sends the bubble to the tile a rows along gx and b columns along gy (a, b in -1, 0, 1); 4 keeps it; 9 marks an empty slot. No bubble leaves the plane. At most 128 bubbles of one tile carry the same code other than 4 and 9, and in every draw each tile sends exactly 128 to one neighbour. Among all bubbles bound for one tile the targets are distinct; for empty slots (code 9) the target is 0 and means nothing. `positions`: A bubble's x lies in [a * 128, (a + 1) * 128] and its y in [b * 16, (b + 1) * 16] for its destination tile (a, b); z lies in [0, 16).
All inputs are finite; a program needn't handle non-finite values.
Results may differ from a plain program's by a relative error of at most 0.0003.
Values sent between devices are 32-bit elements; how exact they have to be, the bound alone decides.
A program may use at most 64 MiB of HBM per device.

v0:
```python
import functools
import math

import jax
import jax.numpy as jnp
from jax import lax
from jax.experimental import pallas as pl
from jax.experimental.pallas import tpu as pltpu
from jax.sharding import PartitionSpec as P

time_step = 0.2
four_pi = 4.0 * math.pi
speed_scale = 1.0 / 16.0
smooth_eps = 3e-6 * speed_scale * speed_scale
flux_unit = 1.0 / (12.0 * speed_scale)

DIRS = [c for c in range(9) if c != 4]
X_DIRS = (1, 7)
Y_DIRS = (3, 5)
DIAG = (0, 2, 6, 8)


def weno_offset(d1, d2, d3, d4):
    t1 = d2 - d1
    t2 = d3 - d2
    t3 = d4 - d3
    d2q = 0.75 * d2
    d3q = 0.75 * d3
    b0 = t1 * t1 + (d2q * (t1 + d2) + smooth_eps)
    b1 = t2 * t2 + (d2q * d3 + smooth_eps)
    b2 = t3 * t3 + (d3q * (d3 - t3) + smooth_eps)
    m0 = b1 * b2
    m1 = b0 * b2
    m2 = b0 * b1
    w0 = m0 * m0
    w1 = 6.0 * (m1 * m1)
    w2 = 3.0 * (m2 * m2)
    a = t1 - t2
    return (w0 * (a + a) + w2 * (t2 - t3)) / (w0 + w1 + w2)


def face_flux(q, u):
    up, down = u
    g = [up[i] * q[i] for i in range(5)]
    h = [down[i] * q[i + 1] for i in range(5)]
    r = [g[i + 1] - g[i] for i in range(4)]
    l = [h[i + 1] - h[i] for i in range(4)]
    mid = r[2] - l[1]
    line = 6.0 * (g[2] + h[2]) + ((r[1] - l[2]) + (mid + mid))
    return line + (weno_offset(*r) - weno_offset(l[3], l[2], l[1], l[0]))


def split_max(u):
    a = [jnp.abs(v) for v in u]
    top = jnp.maximum(
        jnp.maximum(jnp.maximum(a[0], a[1]), jnp.maximum(a[2], a[3])), jnp.maximum(a[4], a[5])
    )
    return [v + top for v in u[:5]], [v - top for v in u[1:]]


def split2(v):
    hi = v.astype(jnp.bfloat16)
    lo = (v - hi.astype(jnp.float32)).astype(jnp.bfloat16)
    return hi, lo


def split3_rows(v):
    hi = v.astype(jnp.bfloat16).astype(jnp.float32)
    rest = v - hi
    mid = rest.astype(jnp.bfloat16).astype(jnp.float32)
    return jnp.concatenate([hi, mid, rest - mid], axis=0)


def tent(d):
    return 0.5 * jnp.maximum(0.0, 1.0 - 0.5 * jnp.abs(d))


def dot(a, b, trans):
    dims = (((1,), (1,)), ((), ())) if trans else (((1,), (0,)), ((), ()))
    return lax.dot_general(a, b, dims, preferred_element_type=jnp.float32)


def kernel(
    n_gx,
    n_gy,
    dims,
    fields_ref,
    vel_ref,
    coup_hbm,
    pos_hbm,
    lr_hbm,
    gr_hbm,
    rg_hbm,
    gp_hbm,
    code_hbm,
    tgt_hbm,
    out_ref,
    bub_ref,
    coup_ref,
    pos_ref,
    lr_ref,
    gr_ref,
    rg_ref,
    gp_ref,
    code_ref,
    tgt_ref,
    small_sem,
    q,
    q1,
    ux,
    s_own,
    s_in,
    c_in,
    s1_own,
    s1_in,
    c1_in,
    outbox,
    inbox,
    vals,
    samp,
    wxh,
    wxl,
    wzy,
    dep,
    depx,
    depc,
    dy_in,
    dx_in,
    dc_in,
    smear,
    eface,
    yface,
    drim,
    stage,
    acc,
    in_sem,
    out_sem,
    send_sem,
    recv_sem,
):
    nf, nz, ny, nx, slots = dims
    f32 = jnp.float32
    me_x = lax.axis_index("gx")
    me_y = lax.axis_index("gy")
    lane = lax.broadcasted_iota(jnp.int32, (nz, nx), 1)
    group = lane // 8
    sub = lane % 8

    def inside(c, sign):
        a, b = sign * (c // 3 - 1), sign * (c % 3 - 1)
        ok = None
        for pos, step, count in ((me_x, a, n_gx), (me_y, b, n_gy)):
            cond = None
            if step == 1:
                cond = pos < count - 1
            elif step == -1:
                cond = pos > 0
            if cond is not None:
                ok = cond if ok is None else jnp.logical_and(ok, cond)
        return ok

    def desc(kind, c, src, dst):
        return pltpu.make_async_remote_copy(
            src_ref=src,
            dst_ref=dst,
            send_sem=send_sem.at[kind, c],
            recv_sem=recv_sem.at[kind, c],
            device_id=(me_x + (c // 3 - 1), me_y + (c % 3 - 1)),
            device_id_type=pl.DeviceIdType.MESH,
        )

    def send(kind, c, src, dst):
        @pl.when(inside(c, 1))
        def _():
            desc(kind, c, src, dst).start()

    def sent(kind, c, src, dst):
        @pl.when(inside(c, 1))
        def _():
            desc(kind, c, src, dst).wait_send()

    def recv(kind, c, src, dst):
        @pl.when(inside(c, -1))
        def _():
            desc(kind, c, src, dst).wait_recv()

        @pl.when(jnp.logical_not(inside(c, -1)))
        def _():
            dst[...] = jnp.zeros(dst.shape, f32)

    def rim_msgs(buf, packed, packed_in, corner_in):
        count = packed.shape[0]
        depth = buf.shape[0]
        yield 3, buf.at[:, pl.ds(3, 3)], buf.at[:, pl.ds(ny + 3, 3)]
        yield 5, buf.at[:, pl.ds(ny, 3)], buf.at[:, pl.ds(0, 3)]
        for n, c in enumerate(X_DIRS):
            yield c, packed, packed_in.at[n]
        for n, c in enumerate(DIAG):
            yield c, packed.at[0], corner_in.at[n]

    def smear_msgs(s):
        yield 3, dep.at[s, pl.ds(0, 2)], dy_in.at[s, 0]
        yield 5, dep.at[s, pl.ds(ny + 2, 2)], dy_in.at[s, 1]
        for n, c in enumerate(X_DIRS):
            yield c, depx.at[s], dx_in.at[s, n]
        for n, c in enumerate(DIAG):
            yield c, depc.at[s], dc_in.at[s, n]

    bubble_msgs = [(c, outbox.at[n], inbox.at[n]) for n, c in enumerate(DIRS)]
    rims0 = list(rim_msgs(q, s_own, s_in, c_in))
    rims1 = list(rim_msgs(q1, s1_own, s1_in, c1_in))
    smears = [list(smear_msgs(0)), list(smear_msgs(1))]

    small = [
        pltpu.make_async_copy(src, dst, small_sem.at[n])
        for n, (src, dst) in enumerate(
            (
                (code_hbm, code_ref),
                (tgt_hbm, tgt_ref),
                (pos_hbm, pos_ref),
                (lr_hbm, lr_ref),
                (gr_hbm, gr_ref),
                (rg_hbm, rg_ref),
                (gp_hbm, gp_ref),
                (coup_hbm, coup_ref),
            )
        )
    ]
    for copy in small:
        copy.start()
    loads = []
    for y in range(ny):
        loads.append(
            pltpu.make_async_copy(
                fields_ref.at[:, :, y, :], q.at[pl.ds(0, nf), y + 3], in_sem.at[3 * y]
            )
        )
        loads.append(
            pltpu.make_async_copy(vel_ref.at[1, :, y, :], q.at[nf, y + 3], in_sem.at[3 * y + 1])
        )
        loads.append(
            pltpu.make_async_copy(vel_ref.at[0, :, y, :], ux.at[y], in_sem.at[3 * y + 2])
        )
    for copy in loads:
        copy.start()

    barrier = pltpu.get_barrier_semaphore()
    neighbours = jnp.int32(0)
    for c in DIRS:
        ok = inside(c, 1)

        @pl.when(ok)
        def _():
            pl.semaphore_signal(
                barrier,
                inc=1,
                device_id=(me_x + (c // 3 - 1), me_y + (c % 3 - 1)),
                device_id_type=pl.DeviceIdType.MESH,
            )

        neighbours = neighbours + ok.astype(jnp.int32)

    for copy in small:
        copy.wait()
    code = code_ref[0]
    target = tgt_ref[0]
    for r in range(3):
        vals[pl.ds(r, 1), :] = pos_ref[r, 0]
    vals[pl.ds(3, 1), :] = lr_ref[0]
    vals[pl.ds(4, 1), :] = gr_ref[0]
    vals[pl.ds(5, 1), :] = rg_ref[0]
    vals[pl.ds(6, 1), :] = gp_ref[0]
    vals[pl.ds(7, 1), :] = (target + 1).astype(f32)
    parts = split3_rows(vals[...])
    row16 = lax.broadcasted_iota(jnp.int32, (16, slots), 0)
    moves = jnp.where((row16 == code) & (row16 != 4) & (row16 < 9), 1.0, 0.0).astype(f32)
    chunks = slots // 128
    stacked = jnp.concatenate(
        [moves[:, 128 * k : 128 * (k + 1)] for k in range(chunks)], axis=0
    )
    upper = lax.broadcasted_iota(jnp.int32, (128, 128), 0) < lax.broadcasted_iota(
        jnp.int32, (128, 128), 1
    )
    before = dot(
        stacked.astype(jnp.bfloat16), jnp.where(upper, 1.0, 0.0).astype(jnp.bfloat16), False
    )
    offset = jnp.zeros((16, 1), f32)
    ranks = []
    for k in range(chunks):
        chunk = stacked[16 * k : 16 * (k + 1)]
        ranks.append(
            jnp.sum(chunk * (before[16 * k : 16 * (k + 1)] + offset), axis=0, keepdims=True)
        )
        offset = offset + jnp.sum(chunk, axis=1, keepdims=True)
    rank = jnp.concatenate(ranks, axis=1)
    row128 = lax.broadcasted_iota(jnp.int32, (128, slots), 0)
    pick = jnp.where(row128.astype(f32) == rank, 1.0, 0.0).astype(jnp.bfloat16)
    masked = jnp.concatenate([jnp.where(code == c, parts, 0.0) for c in DIRS], axis=0)
    boxes = dot(masked.astype(jnp.bfloat16), pick, True)
    for n in range(8):
        outbox[n] = (
            boxes[24 * n : 24 * n + 8] + boxes[24 * n + 8 : 24 * n + 16]
        ) + boxes[24 * n + 16 : 24 * n + 24]

    pl.semaphore_wait(barrier, neighbours)
    for c, src, dst in bubble_msgs:
        send(0, c, src, dst)

    for copy in loads:
        copy.wait()

    def pack_rows(rows):
        packed = jnp.zeros((nz, nx), f32)
        for y, row in rows:
            packed = jnp.where(group == y, pltpu.roll(row, (8 * y + 3) % nx, 1), packed)
        return packed

    for c, src, dst in rims0[:2]:
        send(1, c, src, dst)
    for f in range(nf):
        s_own[f] = pack_rows([(y, q[f, y + 3]) for y in range(ny)])
    s_own[nf] = pack_rows([(y, ux[y]) for y in range(ny)])
    for c, src, dst in rims0[2:]:
        send(1, c, src, dst)

    def y_faces(buf, first, count, skip):
        def body(k, carry):
            y = first + k + jnp.where(k >= 3, skip, 0)
            u = split_max([speed_scale * q[nf, y + 1 + o] for o in range(6)])
            for f in range(nf):
                yface[f, y + 1] = face_flux([buf[f, y + 1 + o] for o in range(6)], u)
            return carry

        lax.fori_loop(0, count, body, 0)

    def inner_faces(buf):
        y_faces(buf, 2, ny - 5, 0)

    def outer_faces(buf):
        y_faces(buf, -1, 6, ny - 5)

    inner_faces(q)

    for c, src, dst in bubble_msgs:
        recv(0, c, src, dst)
    stay = jnp.where(code == 4, vals[...], 0.0)
    all_vals = jnp.concatenate([stay] + [inbox[n] for n in range(8)], axis=1)
    slot = all_vals[7:8].astype(jnp.int32) - 1
    slot_hi = slot >> 7
    slot_lo = slot & 127
    total = all_vals.shape[1]
    place = jnp.where(
        lax.broadcasted_iota(jnp.int32, (128, total), 0) == slot_lo, 1.0, 0.0
    ).astype(jnp.bfloat16)
    all_parts = split3_rows(all_vals)
    spread = jnp.concatenate(
        [jnp.where(slot_hi == h, all_parts, 0.0) for h in range(chunks)], axis=0
    )
    homes = dot(spread.astype(jnp.bfloat16), place, True)
    bubbles = jnp.concatenate(
        [
            (homes[24 * h : 24 * h + 8] + homes[24 * h + 8 : 24 * h + 16])
            + homes[24 * h + 16 : 24 * h + 24]
            for h in range(chunks)
        ],
        axis=1,
    )
    occupied = jnp.where(bubbles[7:8] > 0.5, 1.0, 0.0)
    local_x = bubbles[0:1] - (me_x * nx).astype(f32)
    local_y = bubbles[1:2] - (me_y * ny).astype(f32)
    cell = lax.broadcasted_iota(jnp.int32, (nx, slots), 0)
    rim_cell = jnp.where(cell < nx // 2, cell + nx, cell - nx)
    hi, lo = split2(tent(local_x - (cell.astype(f32) + 0.5)))
    wxh[pl.ds(0, nx)] = hi
    wxl[pl.ds(0, nx)] = lo
    hi, lo = split2(tent(local_x - (rim_cell.astype(f32) + 0.5)))
    wxh[pl.ds(nx, nx)] = hi
    wxl[pl.ds(nx, nx)] = lo
    z_dist = jnp.abs(
        bubbles[2:3] - (lax.broadcasted_iota(jnp.int32, (nz, slots), 0).astype(f32) + 0.5)
    )
    weight_z = tent(jnp.minimum(z_dist, nz - z_dist))
    for ye in range(ny + 4):
        wzy[pl.ds(ye * nz, nz)] = weight_z * tent(local_y - (ye - 1.5))

    rows = (ny + 4) * nz
    step_rows = rows // 4

    def sample_rows(start, count):
        ph, plow = split2(samp[pl.ds(start, count)])
        both = dot(jnp.concatenate([ph, plow], axis=0), wxh[...], False)
        table = both[:count] + both[count:] + dot(ph, wxl[...], False)
        prod = table * wzy[pl.ds(start, count)]
        part = prod[0:8]
        for k in range(1, count // 8):
            part = part + prod[8 * k : 8 * (k + 1)]
        acc[...] += part

    def sampled_rest():
        sample_rows(ny * nz, 4 * nz)
        return jnp.sum(acc[...], axis=0, keepdims=True)

    def deposit(s, volume):
        planes = step_rows // nz

        def body(k, carry):
            part = wzy[pl.ds(pl.multiple_of(k * step_rows, step_rows), step_rows)] * volume
            ph, plow = split2(part)
            both = dot(jnp.concatenate([ph, plow], axis=0), wxh[...], True)
            d = both[:step_rows] + both[step_rows:] + dot(ph, wxl[...], True)
            for r in range(planes):
                dep[s, k * planes + r] = d[r * nz : (r + 1) * nz, :nx]
                drim[k * planes + r] = d[r * nz : (r + 1) * nz, nx:]
            return carry

        lax.fori_loop(0, 4, body, 0)
        rims = [drim[r] for r in range(ny + 4)]
        depx[s] = pack_rows([(y, rims[y + 2]) for y in range(ny)])
        depc[s] = pack_rows(
            [(0, rims[ny + 2]), (1, rims[ny + 3]), (ny - 2, rims[0]), (ny - 1, rims[1])]
        )
        for c, src, dst in smears[s]:
            send(2 + s, c, src, dst)

    def gather_smear(s):
        for c, src, dst in smears[s]:
            recv(2 + s, c, src, dst)
        low = lane < nx // 2
        from_right = dx_in[s, 0] + jnp.where(low, dc_in[s, 1], dc_in[s, 0])
        from_left = dx_in[s, 1] + jnp.where(low, dc_in[s, 3], dc_in[s, 2])
        merged = jnp.where(sub >= 3, from_left, from_right)
        edge = (lane < 2) | (lane >= nx - 2)
        for y in range(ny):
            total_row = dep[s, y + 2] + jnp.where(
                edge, pltpu.roll(merged, (nx - 8 * y - 3) % nx, 1), 0.0
            )
            if y < 2:
                total_row = total_row + dy_in[s, 1, y]
            if y >= ny - 2:
                total_row = total_row + dy_in[s, 0, y - (ny - 2)]
            smear[y] = total_row

    def fill_sample(buf, own, got, corner):
        left = sub < 3
        mid = jnp.where(left, got[1, 0], got[0, 0])
        top = jnp.where(left, corner[3], corner[1])
        bottom = jnp.where(left, corner[2], corner[0])
        for ye in range(ny + 4):
            y = ye - 2
            samp[pl.ds(ye * nz, nz), pl.ds(0, nx)] = buf[0, ye + 1]
            source = top if y < 0 else (bottom if y >= ny else mid)
            home = y + ny if y < 0 else (y - ny if y >= ny else y)
            samp[pl.ds(ye * nz, nz), pl.ds(nx, nx)] = pltpu.roll(
                source, (nx - 8 * home - 3) % nx, 1
            )

    rest_log = bubbles[3:4] + bubbles[5:6]
    pressure_gas = bubbles[6:7]

    def rate_of(s, w, sampled):
        gap = (
            pressure_gas * jnp.exp(-3.0 * (s - rest_log)) - 1.0 - 0.5 * sampled - 0.2 * w
        )
        return gap * jnp.exp(-2.0 * s) - 2.5 * w * w

    def volume_of(s, w):
        return occupied * four_pi * jnp.exp(3.0 * s) * w

    s_zero, w_zero = bubbles[3:4], bubbles[4:5]
    deposit(0, volume_of(s_zero, w_zero))
    def x_windows(x, r):
        return [
            pltpu.roll(jnp.where(lane >= nx - 2, r, x), 2, 1),
            pltpu.roll(jnp.where(lane >= nx - 1, r, x), 1, 1),
            x,
            pltpu.roll(jnp.where(lane < 1, r, x), nx - 1, 1),
            pltpu.roll(jnp.where(lane < 2, r, x), nx - 2, 1),
            pltpu.roll(jnp.where(lane < 3, r, x), nx - 3, 1),
        ]

    def packed_windows(p):
        return [p] + [pltpu.roll(p, nx - o, 1) for o in range(1, 6)]

    def divergence(buf, own, got, emit):
        left = sub < 3
        ue = split_max(packed_windows(speed_scale * jnp.where(left, s_in[1, nf], s_own[nf])))
        for f in range(nf):
            e = face_flux(packed_windows(jnp.where(left, got[1, f], own[f])), ue)
            eface[f] = pltpu.roll(e, 3, 1)
        acc[...] = jnp.zeros((8, slots), f32)

        def body(y, carry):
            sample_rows(pl.multiple_of(y * nz, nz), nz)
            shift = (nx - 3) - 8 * y
            ur = pltpu.roll(jnp.where(left, s_in[1, nf], s_in[0, nf]), shift, 1)
            uxw = split_max([speed_scale * v for v in x_windows(ux[y], ur)])
            for f in range(nf):
                r = pltpu.roll(jnp.where(left, got[1, f], got[0, f]), shift, 1)
                fx = face_flux(x_windows(buf[f, y + 3], r), uxw)
                fx_before = jnp.where(
                    lane == 0, pltpu.roll(eface[f], shift, 1), pltpu.roll(fx, 1, 1)
                )
                emit(f, y, (fx - fx_before) + (yface[f, y + 1] - yface[f, y]))
            return carry

        lax.fori_loop(0, ny, body, 0)

    for c, src, dst in rims0:
        recv(1, c, src, dst)
    fill_sample(q, s_own, s_in, c_in)
    outer_faces(q)

    def emit_one(f, y, div):
        q1[f, y + 3] = q[f, y + 3] - (time_step * flux_unit) * div

    divergence(q, s_own, s_in, emit_one)
    gather_smear(0)
    for y in range(ny):
        source = time_step * smear[y]
        for f in range(nf):
            q1[f, y + 3] = q1[f, y + 3] + coup_ref[f] * source
    for c, src, dst in rims1[:2]:
        send(4, c, src, dst)
    for f in range(nf):
        s1_own[f] = pack_rows([(y, q1[f, y + 3]) for y in range(ny)])
    for c, src, dst in rims1[2:]:
        send(4, c, src, dst)

    s_one = s_zero + time_step * w_zero
    w_one = w_zero + time_step * rate_of(s_zero, w_zero, sampled_rest())
    deposit(1, volume_of(s_one, w_one))
    inner_faces(q1)
    for c, src, dst in rims1:
        recv(4, c, src, dst)
    fill_sample(q1, s1_own, s1_in, c1_in)
    outer_faces(q1)

    def emit_two(f, y, div):
        stage[f, y] = 0.5 * (q[f, y + 3] + q1[f, y + 3]) - (0.5 * time_step * flux_unit) * div

    divergence(q1, s1_own, s1_in, emit_two)
    gather_smear(1)
    stores = []
    for y in range(ny):
        source = (0.5 * time_step) * smear[y]
        for f in range(nf):
            stage[f, y] = stage[f, y] + coup_ref[f] * source
        stores.append(
            pltpu.make_async_copy(stage.at[:, y], out_ref.at[:, :, y, :], out_sem.at[y])
        )
        stores[y].start()
    rate_two = rate_of(s_one, w_one, sampled_rest())
    s_two = 0.5 * s_zero + 0.5 * (s_one + time_step * w_one)
    w_two = 0.5 * w_zero + 0.5 * (w_one + time_step * rate_two)
    bub_ref[0, 0] = s_two * occupied
    bub_ref[1, 0] = w_two * occupied
    for copy in stores:
        copy.wait()

    for kind, msgs in ((0, bubble_msgs), (1, rims0), (2, smears[0]), (3, smears[1]), (4, rims1)):
        for c, src, dst in msgs:
            sent(kind, c, src, dst)


def shards(n_gx, n_gy, fields, velocity, coupling, positions, log_radius, growth, rest_gap,
           gas_pressure, move_codes, targets):
    nf, nz, ny, nx = fields.shape
    slots = move_codes.shape[2]
    vmem = pl.BlockSpec(memory_space=pltpu.VMEM)
    f32 = jnp.float32
    rows = (ny + 4) * nz
    sc = lambda *shape: pltpu.VMEM(shape, f32)
    out, bub = pl.pallas_call(
        functools.partial(kernel, n_gx, n_gy, (nf, nz, ny, nx, slots)),
        out_shape=(
            jax.ShapeDtypeStruct((nf, nz, ny, nx), f32),
            jax.ShapeDtypeStruct((2, 1, 1, slots), f32),
        ),
        in_specs=[pl.BlockSpec(memory_space=pltpu.HBM)] * 10,
        out_specs=(pl.BlockSpec(memory_space=pl.ANY), vmem),
        scratch_shapes=[
            pltpu.SMEM((nf,), f32),
            sc(3, 1, 1, slots),
            sc(1, 1, slots),
            sc(1, 1, slots),
            sc(1, 1, slots),
            sc(1, 1, slots),
            pltpu.VMEM((1, 1, slots), jnp.int32),
            pltpu.VMEM((1, 1, slots), jnp.int32),
            pltpu.SemaphoreType.DMA((8,)),
            sc(nf + 1, ny + 6, nz, nx),
            sc(nf, ny + 6, nz, nx),
            sc(ny, nz, nx),
            sc(nf + 1, nz, nx),
            sc(2, nf + 1, nz, nx),
            sc(4, nz, nx),
            sc(nf, nz, nx),
            sc(2, nf, nz, nx),
            sc(4, nz, nx),
            sc(8, 8, 128),
            sc(8, 8, 128),
            sc(8, slots),
            sc(rows, 2 * nx),
            pltpu.VMEM((2 * nx, slots), jnp.bfloat16),
            pltpu.VMEM((2 * nx, slots), jnp.bfloat16),
            sc(rows, slots),
            sc(2, ny + 4, nz, nx),
            sc(2, nz, nx),
            sc(2, nz, nx),
            sc(2, 2, 2, nz, nx),
            sc(2, 2, nz, nx),
            sc(2, 4, nz, nx),
            sc(ny, nz, nx),
            sc(nf, nz, nx),
            sc(nf, ny + 1, nz, nx),
            sc(ny + 4, nz, nx),
            sc(nf, ny, nz, nx),
            sc(8, slots),
            pltpu.SemaphoreType.DMA((3 * ny,)),
            pltpu.SemaphoreType.DMA((ny,)),
            pltpu.SemaphoreType.DMA((5, 9)),
            pltpu.SemaphoreType.DMA((5, 9)),
        ],
        compiler_params=pltpu.CompilerParams(
            collective_id=0, has_side_effects=True
        ),
    )(fields, velocity, coupling, positions, log_radius, growth, rest_gap, gas_pressure,
      move_codes, targets)
    return out, bub


def solution(mesh):
    placed = (
        P(None, None, "gy", "gx"),
        P(None, None, "gy", "gx"),
        P(),
        P(None, "gx", "gy", None),
        P("gx", "gy", None),
        P("gx", "gy", None),
        P("gx", "gy", None),
        P("gx", "gy", None),
        P("gx", "gy", None),
        P("gx", "gy", None),
    )
    return jax.shard_map(
        functools.partial(shards, mesh.shape["gx"], mesh.shape["gy"]),
        mesh=mesh,
        in_specs=placed,
        out_specs=(P(None, None, "gy", "gx"), P(None, "gx", "gy", None)),
        check_vma=False,
    )
```

profile of v0, /device:TPU:1, one launch (start us, length us, event | category | flops | bytes accessed | tf_op | source)
XLA Modules:
  0.0 38.1 jit_solution(2934541913537223617)
XLA Ops:
  0.6 34.8 %shard_map.113 = (f32[6,16,16,128]{3,2,1,0:T(8,128)}, f32[2,1,1,1024]{3,2,1,0:T(1,128)}) custom-call(f32[6,16,16,128]{3,2,1,0:T(8,128)} %fields_ref.1, f32[2,16,16,128]{3,2,1,0:T(8,128)} %vel_ref.1, f32[6]{0:T(128)} %coup_hbm.1, f32[3,1,1,1024]{3,2,1,0:T(1,128)} %pos_hbm.1, f32[1,1,1024]{2,1,0:T(1,128)} %lr_hbm.1, f32[1,1,1024]{2,1,0:T(1,128)} %gr_hbm.1, ...), custom_call_target="tpu_custom_call" | custom-call | tf_op jit(solution)/shard_map/pallas_call | solution.py:573
  35.4 0.0 copy-start
  35.4 2.1 %copy.14 = f32[6,16,16,128]{3,2,1,0:T(8,128)} copy(f32[6,16,16,128]{3,2,1,0:T(8,128)} %get-tuple-element.4) | data formatting | bytes 1572864
  37.5 0.0 copy-done
  37.5 0.6 %copy.15 = f32[2,1,1,1024]{3,2,1,0:T(1,128)} copy(f32[2,1,1,1024]{3,2,1,0:T(1,128)S(1)} %copy-done) | data formatting | bytes 16384
Async XLA Ops:
  35.4 2.1 %copy-start = (f32[2,1,1,1024]{3,2,1,0:T(1,128)S(1)}, f32[2,1,1,1024]{3,2,1,0:T(1,128)}, u32[]{:S(2)}) copy-start(f32[2,1,1,1024]{3,2,1,0:T(1,128)} %get-tuple-element.5) | copy-start | bytes 24580
where the time goes:
time: 38.3 us; the launch traced here: 38.1 us
  Pallas kernels  34.8 us (91%)
  local copies, waits for them, and re-layouts  2.7 us (7%)
  between operations  0.65 us (2%)
    pallas_call x1, Pallas kernels, shards(): pl.pallas_call(functools.partial(kernel, n_gx, n_gy, (nf, nz, ny, nx, slo...  34.8 us
    unnamed x4, local copies, waits for them, and re-layouts  2.7 us

commit v1 on v0

--- a/solution.py
+++ b/solution.py
@@ -573,11 +573,11 @@
     out, bub = pl.pallas_call(
         functools.partial(kernel, n_gx, n_gy, (nf, nz, ny, nx, slots)),
         out_shape=(
-            jax.ShapeDtypeStruct((nf, nz, ny, nx), f32),
-            jax.ShapeDtypeStruct((2, 1, 1, slots), f32),
+            pltpu.VMEM((nf, nz, ny, nx), f32),
+            pltpu.VMEM((2, 1, 1, slots), f32),
         ),
         in_specs=[pl.BlockSpec(memory_space=pltpu.HBM)] * 10,
-        out_specs=(pl.BlockSpec(memory_space=pl.ANY), vmem),
+        out_specs=(vmem, vmem),
         scratch_shapes=[
             pltpu.SMEM((nf,), f32),
             sc(3, 1, 1, slots),

time: 38.3 us -> 36.6 us (0.956)
  local copies, waits for them, and re-layouts: 2.7 us -> 1.48 us
  Pallas kernels: 34.8 us -> 34.3 us
    unnamed x4 -> x2, local copies, waits for them, and re-layouts: 2.7 us -> 1.48 us
    pallas_call x1, Pallas kernels: 34.8 us -> 34.3 us  [shards(): pl.pallas_call(functools.partial(kernel, n_gx, n_gy, (nf, nz, ny, nx, slo...]
where the time goes in v1:
time: 36.6 us; the launch traced here: 36.4 us
  Pallas kernels  34.3 us (94%)
  local copies, waits for them, and re-layouts  1.48 us (4%)
  between operations  0.64 us (2%)
    pallas_call x1, Pallas kernels, shards(): pl.pallas_call(functools.partial(kernel, n_gx, n_gy, (nf, nz, ny, nx, slo...  34.3 us
    unnamed x2, local copies, waits for them, and re-layouts  1.48 us

profile of v1, /device:TPU:1, one launch (start us, length us, event | category | flops | bytes accessed | tf_op | source)
XLA Modules:
  0.0 36.4 jit_solution(1552749422991829599)
XLA Ops:
  0.6 34.3 %shard_map.113 = (f32[6,16,16,128]{3,2,1,0:T(8,128)S(1)}, f32[2,1,1,1024]{3,2,1,0:T(1,128)S(1)}) custom-call(f32[6,16,16,128]{3,2,1,0:T(8,128)} %fields_ref.1, f32[2,16,16,128]{3,2,1,0:T(8,128)} %vel_ref.1, f32[6]{0:T(128)} %coup_hbm.1, f32[3,1,1,1024]{3,2,1,0:T(1,128)} %pos_hbm.1, f32[1,1,1024]{2,1,0:T(1,128)} %lr_hbm.1, f32[1,1,1024]{2,1,0:T(1,128)} %gr_hbm.1, ...), custom_call_target="tpu_custom_call" | custom-call | tf_op jit(solution)/shard_map/pallas_call | solution.py:573
  34.9 0.9 %copy.14 = f32[6,16,16,128]{3,2,1,0:T(8,128)} copy(f32[6,16,16,128]{3,2,1,0:T(8,128)S(1)} %get-tuple-element.2) | data formatting | bytes 1572864
  35.8 0.6 %copy.15 = f32[2,1,1,1024]{3,2,1,0:T(1,128)} copy(f32[2,1,1,1024]{3,2,1,0:T(1,128)S(1)} %get-tuple-element.3) | data formatting | bytes 16384

commit v2 on v1

--- a/solution.py
+++ b/solution.py
@@ -10,9 +10,8 @@
 
 time_step = 0.2
 four_pi = 4.0 * math.pi
-speed_scale = 1.0 / 16.0
-smooth_eps = 3e-6 * speed_scale * speed_scale
-flux_unit = 1.0 / (12.0 * speed_scale)
+smooth_eps = 3e-6
+flux_unit = 1.0 / 12.0
 
 DIRS = [c for c in range(9) if c != 4]
 X_DIRS = (1, 7)
@@ -20,42 +19,34 @@
 DIAG = (0, 2, 6, 8)
 
 
-def weno_offset(d1, d2, d3, d4):
+def weno_side(d1, d2, d3, d4):
     t1 = d2 - d1
     t2 = d3 - d2
     t3 = d4 - d3
-    d2q = 0.75 * d2
-    d3q = 0.75 * d3
-    b0 = t1 * t1 + (d2q * (t1 + d2) + smooth_eps)
-    b1 = t2 * t2 + (d2q * d3 + smooth_eps)
-    b2 = t3 * t3 + (d3q * (d3 - t3) + smooth_eps)
-    m0 = b1 * b2
-    m1 = b0 * b2
-    m2 = b0 * b1
-    w0 = m0 * m0
-    w1 = 6.0 * (m1 * m1)
-    w2 = 3.0 * (m2 * m2)
-    a = t1 - t2
-    return (w0 * (a + a) + w2 * (t2 - t3)) / (w0 + w1 + w2)
-
-
-def face_flux(q, u):
-    up, down = u
-    g = [up[i] * q[i] for i in range(5)]
-    h = [down[i] * q[i + 1] for i in range(5)]
-    r = [g[i + 1] - g[i] for i in range(4)]
-    l = [h[i + 1] - h[i] for i in range(4)]
-    mid = r[2] - l[1]
-    line = 6.0 * (g[2] + h[2]) + ((r[1] - l[2]) + (mid + mid))
-    return line + (weno_offset(*r) - weno_offset(l[3], l[2], l[1], l[0]))
+    x = 0.75 * d2
+    y = 0.75 * d3
+    b0 = t1 * (t1 + x) + (x * d2 + smooth_eps)
+    b1 = t2 * t2 + (x * d3 + smooth_eps)
+    b2 = t3 * (t3 - y) + (y * d3 + smooth_eps)
+    j1 = b0 / b1
+    j2 = b0 / b2
+    w2 = (1.5 * j2) * j2
+    w1 = (3.0 * j1) * j1
+    return ((t1 - t2) + w2 * (t2 - t3)) / (w2 + w1 + 0.5) - t2
+
+
+def face_flux(dq, df, pair, top):
+    p = [top * d for d in dq]
+    r = [df[i] + p[i] for i in range(4)]
+    l = [df[i + 1] - p[i + 1] for i in range(4)]
+    return 6.0 * pair + (weno_side(*r) - weno_side(l[3], l[2], l[1], l[0]))
 
 
 def split_max(u):
     a = [jnp.abs(v) for v in u]
-    top = jnp.maximum(
+    return jnp.maximum(
         jnp.maximum(jnp.maximum(a[0], a[1]), jnp.maximum(a[2], a[3])), jnp.maximum(a[4], a[5])
     )
-    return [v + top for v in u[:5]], [v - top for v in u[1:]]
 
 
 def split2(v):
@@ -72,7 +63,7 @@
 
 
 def tent(d):
-    return 0.5 * jnp.maximum(0.0, 1.0 - 0.5 * jnp.abs(d))
+    return jnp.maximum(0.0, 0.5 - jnp.abs(0.25 * d))
 
 
 def dot(a, b, trans):
@@ -108,19 +99,29 @@
     q,
     q1,
     ux,
-    s_own,
-    s_in,
+    qt,
+    qt1,
+    topy,
+    topx,
+    dq_s,
+    df_s,
+    pair_s,
+    xface,
+    dv,
+    pk,
+    pk_in,
     c_in,
-    s1_own,
-    s1_in,
+    pk1,
+    pk1_in,
     c1_in,
+    tb,
     outbox,
     inbox,
     vals,
     samp,
-    wxh,
-    wxl,
+    wx,
     wzy,
+    part_s,
     dep,
     depx,
     depc,
@@ -128,11 +129,9 @@
     dx_in,
     dc_in,
     smear,
-    eface,
     yface,
     drim,
     stage,
-    acc,
     in_sem,
     out_sem,
     send_sem,
@@ -189,14 +188,12 @@
             dst[...] = jnp.zeros(dst.shape, f32)
 
     def rim_msgs(buf, packed, packed_in, corner_in):
-        count = packed.shape[0]
-        depth = buf.shape[0]
         yield 3, buf.at[:, pl.ds(3, 3)], buf.at[:, pl.ds(ny + 3, 3)]
         yield 5, buf.at[:, pl.ds(ny, 3)], buf.at[:, pl.ds(0, 3)]
         for n, c in enumerate(X_DIRS):
-            yield c, packed, packed_in.at[n]
+            yield c, packed.at[n], packed_in.at[n]
         for n, c in enumerate(DIAG):
-            yield c, packed.at[0], corner_in.at[n]
+            yield c, packed.at[n // 2, pl.ds(0, 8)], corner_in.at[n]
 
     def smear_msgs(s):
         yield 3, dep.at[s, pl.ds(0, 2)], dy_in.at[s, 0]
@@ -207,8 +204,8 @@
             yield c, depc.at[s], dc_in.at[s, n]
 
     bubble_msgs = [(c, outbox.at[n], inbox.at[n]) for n, c in enumerate(DIRS)]
-    rims0 = list(rim_msgs(q, s_own, s_in, c_in))
-    rims1 = list(rim_msgs(q1, s1_own, s1_in, c1_in))
+    rims0 = list(rim_msgs(q, pk, pk_in, c_in))
+    rims1 = list(rim_msgs(q1, pk1, pk1_in, c1_in))
     smears = [list(smear_msgs(0)), list(smear_msgs(1))]
 
     small = [
@@ -302,44 +299,125 @@
             boxes[24 * n : 24 * n + 8] + boxes[24 * n + 8 : 24 * n + 16]
         ) + boxes[24 * n + 16 : 24 * n + 24]
 
+    half = nz * ny // 128
+    band = ny // half
+    width = 2 * nx
+    early = 5
+
+    def columns(count, body):
+        lax.fori_loop(0, count, lambda n, carry: (body(n), carry)[1], 0)
+
+    def face_rows(buf, first, count, f, z):
+        rows_q = [buf[f, first + i, z] for i in range(count + 5)]
+        flux = [q[nf, first + i, z] * rows_q[i] for i in range(count + 5)]
+        dq = [rows_q[i + 1] - rows_q[i] for i in range(count + 4)]
+        df = [flux[i + 1] - flux[i] for i in range(count + 4)]
+        for j in range(count):
+            yface[f, first + j, z] = face_flux(
+                dq[j : j + 5], df[j : j + 5], flux[j + 2] + flux[j + 3], topy[first + j, z]
+            )
+
+    def y_faces(buf, ranges):
+        def body(n):
+            z = pl.ds(pl.multiple_of((n % (nz // 8)) * 8, 8), 8)
+            for first, count in ranges:
+                face_rows(buf, first, count, n // (nz // 8), z)
+
+        columns(nf * (nz // 8), body)
+
+    def y_tops(first, count):
+        for k in range(first, first + count):
+            topy[k] = split_max([q[nf, k + i] for i in range(6)])
+
+    def x_tops(blocks):
+        for h in range(half):
+            for b in blocks:
+                topx[h, pl.ds(8 * b, 8)] = split_max(
+                    [qt[nf, h, pl.ds(8 * b + 5 + i, 8)] for i in range(6)]
+                )
+
+    def x_cells(buf, f, h, blocks):
+        for b in blocks:
+            at, after = pl.ds(8 * b, 8), pl.ds(8 * b + 1, 8)
+            here, there = buf[f, h, at], buf[f, h, after]
+            flux_here, flux_there = qt[nf, h, at] * here, qt[nf, h, after] * there
+            dq_s[at] = there - here
+            df_s[at] = flux_there - flux_here
+            pair_s[at] = flux_there + flux_here
+
+    def x_faces(f, h, blocks):
+        for b in blocks:
+            dq = [dq_s[pl.ds(8 * b + 5 + i, 8)] for i in range(5)]
+            df = [df_s[pl.ds(8 * b + 5 + i, 8)] for i in range(5)]
+            xface[f, h, pl.ds(8 * b, 8)] = face_flux(
+                dq, df, pair_s[pl.ds(8 * b + 7, 8)], topx[h, pl.ds(8 * b, 8)]
+            )
+
+    last = nx // 8
+
+    def inner_x(buf):
+        def body(n):
+            f, h = n // half, n % half
+            x_cells(buf, f, h, range(1, last + 1))
+            x_faces(f, h, range(1, last - 1))
+
+        columns(nf * half, body)
+
+    def outer_x(buf):
+        def body(n):
+            f, h = n // half, n % half
+            x_cells(buf, f, h, (0, 1, 2, last - 1, last, last + 1))
+            x_faces(f, h, (0, last - 1, last))
+            blocks = [
+                xface[f, h, pl.ds(8 * b + 1, 8)] - xface[f, h, pl.ds(8 * b, 8)]
+                for b in range(last)
+            ]
+            turned = jnp.concatenate(blocks, axis=0).T
+            dv[f, pl.ds(pl.multiple_of(h * band, band), band)] = turned.reshape(band, nz, nx)
+
+        columns(nf * half, body)
+
+    def turn(value):
+        return value.reshape(128, nx).T
+
+    def pack_rims(buf, count, packed):
+        for f in range(count):
+            for h in range(half):
+                to = pl.ds(3 * (f * half + h), 3)
+                packed[0, to] = buf[f, h, pl.ds(8, 3)]
+                packed[1, to] = buf[f, h, pl.ds(nx + 5, 3)]
+
+    def unpack_rims(buf, count, got):
+        for f in range(count):
+            for h in range(half):
+                at = pl.ds(3 * (f * half + h), 3)
+                buf[f, h, pl.ds(nx + 8, 3)] = got[0, at]
+                buf[f, h, pl.ds(5, 3)] = got[1, at]
+
+    wx[pl.ds(nx, nx)] = jnp.zeros((nx, slots), jnp.bfloat16)
+    wx[pl.ds(width + nx, nx)] = jnp.zeros((nx, slots), jnp.bfloat16)
+    wx[pl.ds(2 * width + nx, nx)] = jnp.zeros((nx, slots), jnp.bfloat16)
+    tb[...] = jnp.zeros(tb.shape, f32)
+
+    for copy in loads:
+        copy.wait()
+    for h in range(half):
+        for f in range(nf):
+            qt[f, h, pl.ds(8, nx)] = turn(q[f, pl.ds(3 + h * band, band)])
+        qt[nf, h, pl.ds(8, nx)] = turn(ux[pl.ds(h * band, band)])
+    pack_rims(qt, nf + 1, pk)
+    y_tops(3, ny - 5)
+    y_faces(q, [(3, early)])
+
     pl.semaphore_wait(barrier, neighbours)
     for c, src, dst in bubble_msgs:
         send(0, c, src, dst)
-
-    for copy in loads:
-        copy.wait()
-
-    def pack_rows(rows):
-        packed = jnp.zeros((nz, nx), f32)
-        for y, row in rows:
-            packed = jnp.where(group == y, pltpu.roll(row, (8 * y + 3) % nx, 1), packed)
-        return packed
-
-    for c, src, dst in rims0[:2]:
+    for c, src, dst in rims0:
         send(1, c, src, dst)
-    for f in range(nf):
-        s_own[f] = pack_rows([(y, q[f, y + 3]) for y in range(ny)])
-    s_own[nf] = pack_rows([(y, ux[y]) for y in range(ny)])
-    for c, src, dst in rims0[2:]:
-        send(1, c, src, dst)
-
-    def y_faces(buf, first, count, skip):
-        def body(k, carry):
-            y = first + k + jnp.where(k >= 3, skip, 0)
-            u = split_max([speed_scale * q[nf, y + 1 + o] for o in range(6)])
-            for f in range(nf):
-                yface[f, y + 1] = face_flux([buf[f, y + 1 + o] for o in range(6)], u)
-            return carry
-
-        lax.fori_loop(0, count, body, 0)
-
-    def inner_faces(buf):
-        y_faces(buf, 2, ny - 5, 0)
-
-    def outer_faces(buf):
-        y_faces(buf, -1, 6, ny - 5)
-
-    inner_faces(q)
+
+    x_tops(range(1, last - 1))
+    inner_x(qt)
+    y_faces(q, [(3 + early, ny - 5 - early)])
 
     for c, src, dst in bubble_msgs:
         recv(0, c, src, dst)
@@ -368,14 +446,17 @@
     occupied = jnp.where(bubbles[7:8] > 0.5, 1.0, 0.0)
     local_x = bubbles[0:1] - (me_x * nx).astype(f32)
     local_y = bubbles[1:2] - (me_y * ny).astype(f32)
-    cell = lax.broadcasted_iota(jnp.int32, (nx, slots), 0)
-    rim_cell = jnp.where(cell < nx // 2, cell + nx, cell - nx)
-    hi, lo = split2(tent(local_x - (cell.astype(f32) + 0.5)))
-    wxh[pl.ds(0, nx)] = hi
-    wxl[pl.ds(0, nx)] = lo
-    hi, lo = split2(tent(local_x - (rim_cell.astype(f32) + 0.5)))
-    wxh[pl.ds(nx, nx)] = hi
-    wxl[pl.ds(nx, nx)] = lo
+
+    def put_weight(row, first, count):
+        cell = first + lax.broadcasted_iota(jnp.int32, (count, slots), 0)
+        hi, lo = split2(tent(local_x - (cell.astype(f32) + 0.5)))
+        wx[pl.ds(row, count)] = hi
+        wx[pl.ds(width + row, count)] = hi
+        wx[pl.ds(2 * width + row, count)] = lo
+
+    put_weight(0, 0, nx)
+    put_weight(nx, nx, 16)
+    put_weight(width - 16, -16, 16)
     z_dist = jnp.abs(
         bubbles[2:3] - (lax.broadcasted_iota(jnp.int32, (nz, slots), 0).astype(f32) + 0.5)
     )
@@ -386,35 +467,37 @@
     rows = (ny + 4) * nz
     step_rows = rows // 4
 
-    def sample_rows(start, count):
-        ph, plow = split2(samp[pl.ds(start, count)])
-        both = dot(jnp.concatenate([ph, plow], axis=0), wxh[...], False)
-        table = both[:count] + both[count:] + dot(ph, wxl[...], False)
-        prod = table * wzy[pl.ds(start, count)]
-        part = prod[0:8]
-        for k in range(1, count // 8):
-            part = part + prod[8 * k : 8 * (k + 1)]
-        acc[...] += part
-
-    def sampled_rest():
-        sample_rows(ny * nz, 4 * nz)
-        return jnp.sum(acc[...], axis=0, keepdims=True)
+    def pack_rows(rows):
+        packed = jnp.zeros((nz, nx), f32)
+        for y, row in rows:
+            packed = jnp.where(group == y, pltpu.roll(row, (8 * y + 3) % nx, 1), packed)
+        return packed
+
+    def sampled():
+        sums = []
+        for n in range(slots // 256):
+            at = pl.ds(256 * n, 256)
+            prod = dot(samp[...], wx[:, at], False) * wzy[:, at]
+            part = prod[0:8]
+            for k in range(1, rows // 8):
+                part = part + prod[8 * k : 8 * (k + 1)]
+            sums.append(jnp.sum(part, axis=0, keepdims=True))
+        return jnp.concatenate(sums, axis=1)
 
     def deposit(s, volume):
-        planes = step_rows // nz
-
-        def body(k, carry):
-            part = wzy[pl.ds(pl.multiple_of(k * step_rows, step_rows), step_rows)] * volume
-            ph, plow = split2(part)
-            both = dot(jnp.concatenate([ph, plow], axis=0), wxh[...], True)
-            d = both[:step_rows] + both[step_rows:] + dot(ph, wxl[...], True)
-            for r in range(planes):
-                dep[s, k * planes + r] = d[r * nz : (r + 1) * nz, :nx]
-                drim[k * planes + r] = d[r * nz : (r + 1) * nz, nx:]
-            return carry
-
-        lax.fori_loop(0, 4, body, 0)
-        rims = [drim[r] for r in range(ny + 4)]
+        for k in range(4):
+            at = pl.ds(k * step_rows, step_rows)
+            hi, lo = split2(wzy[at] * volume)
+            part_s[at] = hi
+            part_s[pl.ds(rows + k * step_rows, step_rows)] = lo
+        both = dot(part_s[...], wx[pl.ds(0, width)], True)
+        d = (both[:rows] + both[rows:]) + dot(
+            part_s[pl.ds(0, rows)], wx[pl.ds(2 * width, width)], True
+        )
+        rims = []
+        for r in range(ny + 4):
+            dep[s, r] = d[r * nz : (r + 1) * nz, :nx]
+            rims.append(d[r * nz : (r + 1) * nz, nx:])
         depx[s] = pack_rows([(y, rims[y + 2]) for y in range(ny)])
         depc[s] = pack_rows(
             [(0, rims[ny + 2]), (1, rims[ny + 3]), (ny - 2, rims[0]), (ny - 1, rims[1])]
@@ -440,26 +523,38 @@
                 total_row = total_row + dy_in[s, 0, y - (ny - 2)]
             smear[y] = total_row
 
-    def fill_sample(buf, own, got, corner):
-        left = sub < 3
-        mid = jnp.where(left, got[1, 0], got[0, 0])
-        top = jnp.where(left, corner[3], corner[1])
-        bottom = jnp.where(left, corner[2], corner[0])
+    def put_sample(row, col, value):
+        hi, lo = split2(value)
+        count = value.shape[0]
+        samp[pl.ds(row, count), pl.ds(col, nx)] = hi
+        samp[pl.ds(row, count), pl.ds(width + col, nx)] = lo
+        samp[pl.ds(row, count), pl.ds(2 * width + col, nx)] = hi
+
+    def fill_sample(buf, buft, corner):
         for ye in range(ny + 4):
-            y = ye - 2
-            samp[pl.ds(ye * nz, nz), pl.ds(0, nx)] = buf[0, ye + 1]
-            source = top if y < 0 else (bottom if y >= ny else mid)
-            home = y + ny if y < 0 else (y - ny if y >= ny else y)
-            samp[pl.ds(ye * nz, nz), pl.ds(nx, nx)] = pltpu.roll(
-                source, (nx - 8 * home - 3) % nx, 1
-            )
+            put_sample(ye * nz, 0, buf[0, ye + 1])
+        lanes = lax.broadcasted_iota(jnp.int32, (3, 128), 1)
+        top = lanes >= 128 - 2 * nz
+        final = 3 * (half - 1)
+        for h in range(half):
+            tb[h, pl.ds(0, 3)] = buft[0, h, pl.ds(nx + 8, 3)]
+            tb[h, pl.ds(nx - 3, 3)] = buft[0, h, pl.ds(5, 3)]
+        tb[half, pl.ds(0, 3)] = jnp.where(top, corner[1, pl.ds(final, 3)], corner[0, pl.ds(0, 3)])
+        tb[half, pl.ds(nx - 3, 3)] = jnp.where(
+            top, corner[3, pl.ds(final, 3)], corner[2, pl.ds(0, 3)]
+        )
+        for h in range(half):
+            put_sample(2 * nz + 128 * h, nx, tb[h].T)
+        turned = tb[half].T
+        put_sample(0, nx, turned[128 - 2 * nz :])
+        put_sample((ny + 2) * nz, nx, turned[: 2 * nz])
 
     rest_log = bubbles[3:4] + bubbles[5:6]
     pressure_gas = bubbles[6:7]
 
-    def rate_of(s, w, sampled):
+    def rate_of(s, w, sampled_field):
         gap = (
-            pressure_gas * jnp.exp(-3.0 * (s - rest_log)) - 1.0 - 0.5 * sampled - 0.2 * w
+            pressure_gas * jnp.exp(-3.0 * (s - rest_log)) - 1.0 - 0.5 * sampled_field - 0.2 * w
         )
         return gap * jnp.exp(-2.0 * s) - 2.5 * w * w
 
@@ -468,92 +563,62 @@
 
     s_zero, w_zero = bubbles[3:4], bubbles[4:5]
     deposit(0, volume_of(s_zero, w_zero))
-    def x_windows(x, r):
-        return [
-            pltpu.roll(jnp.where(lane >= nx - 2, r, x), 2, 1),
-            pltpu.roll(jnp.where(lane >= nx - 1, r, x), 1, 1),
-            x,
-            pltpu.roll(jnp.where(lane < 1, r, x), nx - 1, 1),
-            pltpu.roll(jnp.where(lane < 2, r, x), nx - 2, 1),
-            pltpu.roll(jnp.where(lane < 3, r, x), nx - 3, 1),
-        ]
-
-    def packed_windows(p):
-        return [p] + [pltpu.roll(p, nx - o, 1) for o in range(1, 6)]
-
-    def divergence(buf, own, got, emit):
-        left = sub < 3
-        ue = split_max(packed_windows(speed_scale * jnp.where(left, s_in[1, nf], s_own[nf])))
-        for f in range(nf):
-            e = face_flux(packed_windows(jnp.where(left, got[1, f], own[f])), ue)
-            eface[f] = pltpu.roll(e, 3, 1)
-        acc[...] = jnp.zeros((8, slots), f32)
-
-        def body(y, carry):
-            sample_rows(pl.multiple_of(y * nz, nz), nz)
-            shift = (nx - 3) - 8 * y
-            ur = pltpu.roll(jnp.where(left, s_in[1, nf], s_in[0, nf]), shift, 1)
-            uxw = split_max([speed_scale * v for v in x_windows(ux[y], ur)])
-            for f in range(nf):
-                r = pltpu.roll(jnp.where(left, got[1, f], got[0, f]), shift, 1)
-                fx = face_flux(x_windows(buf[f, y + 3], r), uxw)
-                fx_before = jnp.where(
-                    lane == 0, pltpu.roll(eface[f], shift, 1), pltpu.roll(fx, 1, 1)
-                )
-                emit(f, y, (fx - fx_before) + (yface[f, y + 1] - yface[f, y]))
-            return carry
-
-        lax.fori_loop(0, ny, body, 0)
 
     for c, src, dst in rims0:
         recv(1, c, src, dst)
-    fill_sample(q, s_own, s_in, c_in)
-    outer_faces(q)
-
-    def emit_one(f, y, div):
-        q1[f, y + 3] = q[f, y + 3] - (time_step * flux_unit) * div
-
-    divergence(q, s_own, s_in, emit_one)
+    unpack_rims(qt, nf + 1, pk_in)
+    fill_sample(q, qt, c_in)
+    s_one = s_zero + time_step * w_zero
+    w_one = w_zero + time_step * rate_of(s_zero, w_zero, sampled())
+    deposit(1, volume_of(s_one, w_one))
+
+    y_tops(0, 3)
+    y_tops(ny - 2, 3)
+    x_tops((0, last - 1, last))
+    y_faces(q, [(0, 3), (ny - 2, 3)])
+    outer_x(qt)
+
     gather_smear(0)
     for y in range(ny):
         source = time_step * smear[y]
         for f in range(nf):
-            q1[f, y + 3] = q1[f, y + 3] + coup_ref[f] * source
+            div = dv[f, y] + (yface[f, y + 1] - yface[f, y])
+            q1[f, y + 3] = (q[f, y + 3] - (time_step * flux_unit) * div) + coup_ref[f] * source
     for c, src, dst in rims1[:2]:
         send(4, c, src, dst)
-    for f in range(nf):
-        s1_own[f] = pack_rows([(y, q1[f, y + 3]) for y in range(ny)])
+    for h in range(half):
+        for f in range(nf):
+            qt1[f, h, pl.ds(8, nx)] = turn(q1[f, pl.ds(3 + h * band, band)])
+    pack_rims(qt1, nf, pk1)
     for c, src, dst in rims1[2:]:
         send(4, c, src, dst)
 
-    s_one = s_zero + time_step * w_zero
-    w_one = w_zero + time_step * rate_of(s_zero, w_zero, sampled_rest())
-    deposit(1, volume_of(s_one, w_one))
-    inner_faces(q1)
+    inner_x(qt1)
+    y_faces(q1, [(3, ny - 5)])
     for c, src, dst in rims1:
         recv(4, c, src, dst)
-    fill_sample(q1, s1_own, s1_in, c1_in)
-    outer_faces(q1)
-
-    def emit_two(f, y, div):
-        stage[f, y] = 0.5 * (q[f, y + 3] + q1[f, y + 3]) - (0.5 * time_step * flux_unit) * div
-
-    divergence(q1, s1_own, s1_in, emit_two)
+    unpack_rims(qt1, nf, pk1_in)
+    fill_sample(q1, qt1, c1_in)
+    rate_two = rate_of(s_one, w_one, sampled())
+    s_two = 0.5 * s_zero + 0.5 * (s_one + time_step * w_one)
+    w_two = 0.5 * w_zero + 0.5 * (w_one + time_step * rate_two)
+    bub_ref[0, 0] = s_two * occupied
+    bub_ref[1, 0] = w_two * occupied
+    y_faces(q1, [(0, 3), (ny - 2, 3)])
+    outer_x(qt1)
     gather_smear(1)
     stores = []
     for y in range(ny):
         source = (0.5 * time_step) * smear[y]
         for f in range(nf):
-            stage[f, y] = stage[f, y] + coup_ref[f] * source
+            div = dv[f, y] + (yface[f, y + 1] - yface[f, y])
+            stage[f, y] = (
+                0.5 * (q[f, y + 3] + q1[f, y + 3]) - (0.5 * time_step * flux_unit) * div
+            ) + coup_ref[f] * source
         stores.append(
             pltpu.make_async_copy(stage.at[:, y], out_ref.at[:, :, y, :], out_sem.at[y])
         )
         stores[y].start()
-    rate_two = rate_of(s_one, w_one, sampled_rest())
-    s_two = 0.5 * s_zero + 0.5 * (s_one + time_step * w_one)
-    w_two = 0.5 * w_zero + 0.5 * (w_one + time_step * rate_two)
-    bub_ref[0, 0] = s_two * occupied
-    bub_ref[1, 0] = w_two * occupied
     for copy in stores:
         copy.wait()
 
@@ -569,6 +634,9 @@
     vmem = pl.BlockSpec(memory_space=pltpu.VMEM)
     f32 = jnp.float32
     rows = (ny + 4) * nz
+    half = nz * ny // 128
+    deep = nx + 24
+    packed = -(-3 * half * (nf + 1) // 8) * 8
     sc = lambda *shape: pltpu.VMEM(shape, f32)
     out, bub = pl.pallas_call(
         functools.partial(kernel, n_gx, n_gy, (nf, nz, ny, nx, slots)),
@@ -591,19 +659,29 @@
             sc(nf + 1, ny + 6, nz, nx),
             sc(nf, ny + 6, nz, nx),
             sc(ny, nz, nx),
-            sc(nf + 1, nz, nx),
-            sc(2, nf + 1, nz, nx),
-            sc(4, nz, nx),
-            sc(nf, nz, nx),
-            sc(2, nf, nz, nx),
-            sc(4, nz, nx),
+            sc(nf + 1, half, deep, 128),
+            sc(nf, half, deep, 128),
+            sc(ny + 1, nz, nx),
+            sc(half, nx + 8, 128),
+            sc(deep, 128),
+            sc(deep, 128),
+            sc(deep, 128),
+            sc(nf, half, nx + 16, 128),
+            sc(nf, ny, nz, nx),
+            sc(2, packed, 128),
+            sc(2, packed, 128),
+            sc(4, 8, 128),
+            sc(2, packed, 128),
+            sc(2, packed, 128),
+            sc(4, 8, 128),
+            sc(half + 1, 128, 128),
             sc(8, 8, 128),
             sc(8, 8, 128),
             sc(8, slots),
-            sc(rows, 2 * nx),
-            pltpu.VMEM((2 * nx, slots), jnp.bfloat16),
-            pltpu.VMEM((2 * nx, slots), jnp.bfloat16),
+            pltpu.VMEM((rows, 6 * nx), jnp.bfloat16),
+            pltpu.VMEM((6 * nx, slots), jnp.bfloat16),
             sc(rows, slots),
+            pltpu.VMEM((2 * rows, slots), jnp.bfloat16),
             sc(2, ny + 4, nz, nx),
             sc(2, nz, nx),
             sc(2, nz, nx),
@@ -611,11 +689,9 @@
             sc(2, 2, nz, nx),
             sc(2, 4, nz, nx),
             sc(ny, nz, nx),
-            sc(nf, nz, nx),
             sc(nf, ny + 1, nz, nx),
             sc(ny + 4, nz, nx),
             sc(nf, ny, nz, nx),
-            sc(8, slots),
             pltpu.SemaphoreType.DMA((3 * ny,)),
             pltpu.SemaphoreType.DMA((ny,)),
             pltpu.SemaphoreType.DMA((5, 9)),

time: 36.6 us -> 29.2 us (0.80)
  Pallas kernels: 34.3 us -> 26.8 us
    pallas_call x1, Pallas kernels: 34.3 us -> 26.8 us  [shards(): pl.pallas_call(functools.partial(kernel, n_gx, n_gy, (nf, nz, ny, nx, slo...]
where the time goes in v2:
time: 29.2 us; the launch traced here: 29 us
  Pallas kernels  26.8 us (92%)
  local copies, waits for them, and re-layouts  1.48 us (5%)
  between operations  0.64 us (2%)
    pallas_call x1, Pallas kernels, shards(): pl.pallas_call(functools.partial(kernel, n_gx, n_gy, (nf, nz, ny, nx, slo...  26.8 us
    unnamed x2, local copies, waits for them, and re-layouts  1.48 us

profile of v2, /device:TPU:1, one launch (start us, length us, event | category | flops | bytes accessed | tf_op | source)
XLA Modules:
  0.0 29.0 jit_solution(17587391599443005870)
XLA Ops:
  0.6 26.8 %shard_map.113 = (f32[6,16,16,128]{3,2,1,0:T(8,128)S(1)}, f32[2,1,1,1024]{3,2,1,0:T(1,128)S(1)}) custom-call(f32[6,16,16,128]{3,2,1,0:T(8,128)} %fields_ref.1, f32[2,16,16,128]{3,2,1,0:T(8,128)} %vel_ref.1, f32[6]{0:T(128)} %coup_hbm.1, f32[3,1,1,1024]{3,2,1,0:T(1,128)} %pos_hbm.1, f32[1,1,1024]{2,1,0:T(1,128)} %lr_hbm.1, f32[1,1,1024]{2,1,0:T(1,128)} %gr_hbm.1, ...), custom_call_target="tpu_custom_call" | custom-call | tf_op jit(solution)/shard_map/pallas_call | solution.py:641
  27.5 0.9 %copy.14 = f32[6,16,16,128]{3,2,1,0:T(8,128)} copy(f32[6,16,16,128]{3,2,1,0:T(8,128)S(1)} %get-tuple-element.2) | data formatting | bytes 1572864
  28.4 0.6 %copy.15 = f32[2,1,1,1024]{3,2,1,0:T(1,128)} copy(f32[2,1,1,1024]{3,2,1,0:T(1,128)S(1)} %get-tuple-element.3) | data formatting | bytes 16384

commit v3 on v2

--- a/solution.py
+++ b/solution.py
@@ -17,6 +17,7 @@
 X_DIRS = (1, 7)
 Y_DIRS = (3, 5)
 DIAG = (0, 2, 6, 8)
+pieces = 3
 
 
 def weno_side(d1, d2, d3, d4):
@@ -128,12 +129,8 @@
     dy_in,
     dx_in,
     dc_in,
-    smear,
     yface,
-    drim,
-    stage,
     in_sem,
-    out_sem,
     send_sem,
     recv_sem,
 ):
@@ -187,9 +184,12 @@
         def _():
             dst[...] = jnp.zeros(dst.shape, f32)
 
-    def rim_msgs(buf, packed, packed_in, corner_in):
-        yield 3, buf.at[:, pl.ds(3, 3)], buf.at[:, pl.ds(ny + 3, 3)]
-        yield 5, buf.at[:, pl.ds(ny, 3)], buf.at[:, pl.ds(0, 3)]
+    def y_msgs(buf, first, count):
+        f = pl.ds(first, count)
+        yield 3, buf.at[f, pl.ds(3, 3)], buf.at[f, pl.ds(ny + 3, 3)]
+        yield 5, buf.at[f, pl.ds(ny, 3)], buf.at[f, pl.ds(0, 3)]
+
+    def rim_msgs(packed, packed_in, corner_in):
         for n, c in enumerate(X_DIRS):
             yield c, packed.at[n], packed_in.at[n]
         for n, c in enumerate(DIAG):
@@ -204,8 +204,12 @@
             yield c, depc.at[s], dc_in.at[s, n]
 
     bubble_msgs = [(c, outbox.at[n], inbox.at[n]) for n, c in enumerate(DIRS)]
-    rims0 = list(rim_msgs(q, pk, pk_in, c_in))
-    rims1 = list(rim_msgs(q1, pk1, pk1_in, c1_in))
+    rims0 = list(rim_msgs(pk, pk_in, c_in))
+    rims1 = list(rim_msgs(pk1, pk1_in, c1_in))
+    group_of = nf // pieces
+    y_rims0 = [list(y_msgs(q, p * group_of, group_of)) for p in range(pieces)]
+    y_rims1 = [list(y_msgs(q1, p * group_of, group_of)) for p in range(pieces)]
+    y_speed = list(y_msgs(q, nf, 1))
     smears = [list(smear_msgs(0)), list(smear_msgs(1))]
 
     small = [
@@ -302,10 +306,8 @@
     half = nz * ny // 128
     band = ny // half
     width = 2 * nx
-    early = 5
-
-    def columns(count, body):
-        lax.fori_loop(0, count, lambda n, carry: (body(n), carry)[1], 0)
+    lanes_at_once = 3
+    tiles = slots // 256
 
     def face_rows(buf, first, count, f, z):
         rows_q = [buf[f, first + i, z] for i in range(count + 5)]
@@ -317,14 +319,6 @@
                 dq[j : j + 5], df[j : j + 5], flux[j + 2] + flux[j + 3], topy[first + j, z]
             )
 
-    def y_faces(buf, ranges):
-        def body(n):
-            z = pl.ds(pl.multiple_of((n % (nz // 8)) * 8, 8), 8)
-            for first, count in ranges:
-                face_rows(buf, first, count, n // (nz // 8), z)
-
-        columns(nf * (nz // 8), body)
-
     def y_tops(first, count):
         for k in range(first, first + count):
             topy[k] = split_max([q[nf, k + i] for i in range(6)])
@@ -336,7 +330,7 @@
                     [qt[nf, h, pl.ds(8 * b + 5 + i, 8)] for i in range(6)]
                 )
 
-    def x_cells(buf, f, h, blocks):
+    def x_cells(buf, f, h, blocks, dq_s, df_s, pair_s):
         for b in blocks:
             at, after = pl.ds(8 * b, 8), pl.ds(8 * b + 1, 8)
             here, there = buf[f, h, at], buf[f, h, after]
@@ -345,7 +339,7 @@
             df_s[at] = flux_there - flux_here
             pair_s[at] = flux_there + flux_here
 
-    def x_faces(f, h, blocks):
+    def x_faces(f, h, blocks, dq_s, df_s, pair_s):
         for b in blocks:
             dq = [dq_s[pl.ds(8 * b + 5 + i, 8)] for i in range(5)]
             df = [df_s[pl.ds(8 * b + 5 + i, 8)] for i in range(5)]
@@ -355,27 +349,45 @@
 
     last = nx // 8
 
-    def inner_x(buf):
-        def body(n):
-            f, h = n // half, n % half
-            x_cells(buf, f, h, range(1, last + 1))
-            x_faces(f, h, range(1, last - 1))
-
-        columns(nf * half, body)
-
-    def outer_x(buf):
-        def body(n):
-            f, h = n // half, n % half
-            x_cells(buf, f, h, (0, 1, 2, last - 1, last, last + 1))
-            x_faces(f, h, (0, last - 1, last))
-            blocks = [
-                xface[f, h, pl.ds(8 * b + 1, 8)] - xface[f, h, pl.ds(8 * b, 8)]
-                for b in range(last)
-            ]
-            turned = jnp.concatenate(blocks, axis=0).T
-            dv[f, pl.ds(pl.multiple_of(h * band, band), band)] = turned.reshape(band, nz, nx)
-
-        columns(nf * half, body)
+    def halves(h):
+        return pl.ds(pl.multiple_of(h * 8, 8), 8)
+
+    def inner_columns(buf, buft, first, stop):
+        def body(k, carry):
+            for j in range(lanes_at_once):
+                n = k * lanes_at_once + j
+                f, h = n // half, n % half
+                work = (dq_s.at[j], df_s.at[j], pair_s.at[j])
+                x_cells(buft, f, h, range(1, last + 1), *work)
+                x_faces(f, h, range(1, last - 1), *work)
+                face_rows(buf, 3, ny - 5, f, halves(h))
+            return carry
+
+        lax.fori_loop(first, stop, body, 0)
+
+    def outer_column(buf, buft, f, h, slot):
+        work = (dq_s.at[slot], df_s.at[slot], pair_s.at[slot])
+        x_cells(buft, f, h, (0, 1, 2, last - 1, last, last + 1), *work)
+        x_faces(f, h, (0, last - 1, last), *work)
+        blocks = [
+            xface[f, h, pl.ds(8 * b + 1, 8)] - xface[f, h, pl.ds(8 * b, 8)] for b in range(last)
+        ]
+        turned = jnp.concatenate(blocks, axis=0).T
+        dv[f, pl.ds(h * band, band)] = turned.reshape(band, nz, nx)
+        face_rows(buf, 0, 3, f, halves(h))
+        face_rows(buf, ny - 2, 3, f, halves(h))
+
+    def outer_columns(buf, buft, y_rims, kind):
+        sums = []
+        for p in range(pieces):
+            if p:
+                for c, src, dst in y_rims[p]:
+                    recv(kind + p, c, src, dst)
+            for n in range(p * group_of * half, (p + 1) * group_of * half):
+                outer_column(buf, buft, n // half, n % half, n % 4)
+            for n in range(p * tiles // pieces, (p + 1) * tiles // pieces):
+                sums.append(sample_tile(n))
+        return jnp.concatenate(sums, axis=1)
 
     def turn(value):
         return value.reshape(128, nx).T
@@ -407,17 +419,23 @@
         qt[nf, h, pl.ds(8, nx)] = turn(ux[pl.ds(h * band, band)])
     pack_rims(qt, nf + 1, pk)
     y_tops(3, ny - 5)
-    y_faces(q, [(3, early)])
+    x_tops(range(1, last - 1))
+    inner_columns(q, qt, 0, 1)
 
     pl.semaphore_wait(barrier, neighbours)
     for c, src, dst in bubble_msgs:
         send(0, c, src, dst)
+    for c, src, dst in y_speed:
+        send(8, c, src, dst)
+    for c, src, dst in y_rims0[0]:
+        send(5, c, src, dst)
     for c, src, dst in rims0:
         send(1, c, src, dst)
-
-    x_tops(range(1, last - 1))
-    inner_x(qt)
-    y_faces(q, [(3 + early, ny - 5 - early)])
+    for p in range(1, pieces):
+        for c, src, dst in y_rims0[p]:
+            send(5 + p, c, src, dst)
+
+    inner_columns(q, qt, 1, nf * half // lanes_at_once)
 
     for c, src, dst in bubble_msgs:
         recv(0, c, src, dst)
@@ -473,16 +491,13 @@
             packed = jnp.where(group == y, pltpu.roll(row, (8 * y + 3) % nx, 1), packed)
         return packed
 
-    def sampled():
-        sums = []
-        for n in range(slots // 256):
-            at = pl.ds(256 * n, 256)
-            prod = dot(samp[...], wx[:, at], False) * wzy[:, at]
-            part = prod[0:8]
-            for k in range(1, rows // 8):
-                part = part + prod[8 * k : 8 * (k + 1)]
-            sums.append(jnp.sum(part, axis=0, keepdims=True))
-        return jnp.concatenate(sums, axis=1)
+    def sample_tile(n):
+        at = pl.ds(256 * n, 256)
+        prod = dot(samp[...], wx[:, at], False) * wzy[:, at]
+        part = prod[0:8]
+        for k in range(1, rows // 8):
+            part = part + prod[8 * k : 8 * (k + 1)]
+        return jnp.sum(part, axis=0, keepdims=True)
 
     def deposit(s, volume):
         for k in range(4):
@@ -511,17 +526,18 @@
         low = lane < nx // 2
         from_right = dx_in[s, 0] + jnp.where(low, dc_in[s, 1], dc_in[s, 0])
         from_left = dx_in[s, 1] + jnp.where(low, dc_in[s, 3], dc_in[s, 2])
-        merged = jnp.where(sub >= 3, from_left, from_right)
+        return jnp.where(sub >= 3, from_left, from_right)
+
+    def smear_row(s, merged, y):
         edge = (lane < 2) | (lane >= nx - 2)
-        for y in range(ny):
-            total_row = dep[s, y + 2] + jnp.where(
-                edge, pltpu.roll(merged, (nx - 8 * y - 3) % nx, 1), 0.0
-            )
-            if y < 2:
-                total_row = total_row + dy_in[s, 1, y]
-            if y >= ny - 2:
-                total_row = total_row + dy_in[s, 0, y - (ny - 2)]
-            smear[y] = total_row
+        total_row = dep[s, y + 2] + jnp.where(
+            edge, pltpu.roll(merged, (nx - 8 * y - 3) % nx, 1), 0.0
+        )
+        if y < 2:
+            total_row = total_row + dy_in[s, 1, y]
+        if y >= ny - 2:
+            total_row = total_row + dy_in[s, 0, y - (ny - 2)]
+        return total_row
 
     def put_sample(row, col, value):
         hi, lo = split2(value)
@@ -564,67 +580,82 @@
     s_zero, w_zero = bubbles[3:4], bubbles[4:5]
     deposit(0, volume_of(s_zero, w_zero))
 
+    for c, src, dst in y_speed:
+        recv(8, c, src, dst)
     for c, src, dst in rims0:
         recv(1, c, src, dst)
+    for c, src, dst in y_rims0[0]:
+        recv(5, c, src, dst)
     unpack_rims(qt, nf + 1, pk_in)
     fill_sample(q, qt, c_in)
-    s_one = s_zero + time_step * w_zero
-    w_one = w_zero + time_step * rate_of(s_zero, w_zero, sampled())
-    deposit(1, volume_of(s_one, w_one))
-
     y_tops(0, 3)
     y_tops(ny - 2, 3)
     x_tops((0, last - 1, last))
-    y_faces(q, [(0, 3), (ny - 2, 3)])
-    outer_x(qt)
-
-    gather_smear(0)
-    for y in range(ny):
-        source = time_step * smear[y]
+    sampled = outer_columns(q, qt, y_rims0, 5)
+    s_one = s_zero + time_step * w_zero
+    w_one = w_zero + time_step * rate_of(s_zero, w_zero, sampled)
+    deposit(1, volume_of(s_one, w_one))
+
+    merged = gather_smear(0)
+
+    def first_section(y):
+        source = time_step * smear_row(0, merged, y)
         for f in range(nf):
             div = dv[f, y] + (yface[f, y + 1] - yface[f, y])
             q1[f, y + 3] = (q[f, y + 3] - (time_step * flux_unit) * div) + coup_ref[f] * source
-    for c, src, dst in rims1[:2]:
-        send(4, c, src, dst)
+
+    outermost = [0, 1, 2, ny - 3, ny - 2, ny - 1]
+    for y in outermost:
+        first_section(y)
+    for p in range(pieces):
+        for c, src, dst in y_rims1[p]:
+            send(9 + p, c, src, dst)
+    for y in range(3, ny - 3):
+        first_section(y)
     for h in range(half):
         for f in range(nf):
             qt1[f, h, pl.ds(8, nx)] = turn(q1[f, pl.ds(3 + h * band, band)])
     pack_rims(qt1, nf, pk1)
-    for c, src, dst in rims1[2:]:
+    for c, src, dst in rims1:
         send(4, c, src, dst)
 
-    inner_x(qt1)
-    y_faces(q1, [(3, ny - 5)])
+    inner_columns(q1, qt1, 0, nf * half // lanes_at_once)
     for c, src, dst in rims1:
         recv(4, c, src, dst)
+    for c, src, dst in y_rims1[0]:
+        recv(9, c, src, dst)
     unpack_rims(qt1, nf, pk1_in)
     fill_sample(q1, qt1, c1_in)
-    rate_two = rate_of(s_one, w_one, sampled())
+    rate_two = rate_of(s_one, w_one, outer_columns(q1, qt1, y_rims1, 9))
     s_two = 0.5 * s_zero + 0.5 * (s_one + time_step * w_one)
     w_two = 0.5 * w_zero + 0.5 * (w_one + time_step * rate_two)
     bub_ref[0, 0] = s_two * occupied
     bub_ref[1, 0] = w_two * occupied
-    y_faces(q1, [(0, 3), (ny - 2, 3)])
-    outer_x(qt1)
-    gather_smear(1)
-    stores = []
+    merged1 = gather_smear(1)
     for y in range(ny):
-        source = (0.5 * time_step) * smear[y]
+        source = (0.5 * time_step) * smear_row(1, merged1, y)
         for f in range(nf):
             div = dv[f, y] + (yface[f, y + 1] - yface[f, y])
-            stage[f, y] = (
+            out_ref[f, y] = (
                 0.5 * (q[f, y + 3] + q1[f, y + 3]) - (0.5 * time_step * flux_unit) * div
             ) + coup_ref[f] * source
-        stores.append(
-            pltpu.make_async_copy(stage.at[:, y], out_ref.at[:, :, y, :], out_sem.at[y])
-        )
-        stores[y].start()
-    for copy in stores:
-        copy.wait()
-
-    for kind, msgs in ((0, bubble_msgs), (1, rims0), (2, smears[0]), (3, smears[1]), (4, rims1)):
+
+    for kind, msgs in ((0, bubble_msgs), (1, rims0), (2, smears[0]), (3, smears[1]), (4, rims1),
+                       *((5 + p, y_rims0[p]) for p in range(pieces)), (8, y_speed),
+                       *((9 + p, y_rims1[p]) for p in range(pieces))):
         for c, src, dst in msgs:
             sent(kind, c, src, dst)
+
+
+def write_out(fields_ref, bubbles_ref, out_ref, bub_ref, sem):
+    ny = fields_ref.shape[1]
+    copies = [pltpu.make_async_copy(bubbles_ref, bub_ref, sem.at[ny])]
+    for y in range(ny):
+        copies.append(pltpu.make_async_copy(fields_ref.at[:, y], out_ref.at[:, :, y, :], sem.at[y]))
+    for copy in copies:
+        copy.start()
+    for copy in copies:
+        copy.wait()
 
 
 def shards(n_gx, n_gy, fields, velocity, coupling, positions, log_radius, growth, rest_gap,
@@ -641,7 +672,7 @@
     out, bub = pl.pallas_call(
         functools.partial(kernel, n_gx, n_gy, (nf, nz, ny, nx, slots)),
         out_shape=(
-            pltpu.VMEM((nf, nz, ny, nx), f32),
+            pltpu.VMEM((nf, ny, nz, nx), f32),
             pltpu.VMEM((2, 1, 1, slots), f32),
         ),
         in_specs=[pl.BlockSpec(memory_space=pltpu.HBM)] * 10,
@@ -663,9 +694,9 @@
             sc(nf, half, deep, 128),
             sc(ny + 1, nz, nx),
             sc(half, nx + 8, 128),
-            sc(deep, 128),
-            sc(deep, 128),
-            sc(deep, 128),
+            sc(4, deep, 128),
+            sc(4, deep, 128),
+            sc(4, deep, 128),
             sc(nf, half, nx + 16, 128),
             sc(nf, ny, nz, nx),
             sc(2, packed, 128),
@@ -688,21 +719,27 @@
             sc(2, 2, 2, nz, nx),
             sc(2, 2, nz, nx),
             sc(2, 4, nz, nx),
-            sc(ny, nz, nx),
             sc(nf, ny + 1, nz, nx),
-            sc(ny + 4, nz, nx),
-            sc(nf, ny, nz, nx),
             pltpu.SemaphoreType.DMA((3 * ny,)),
-            pltpu.SemaphoreType.DMA((ny,)),
-            pltpu.SemaphoreType.DMA((5, 9)),
-            pltpu.SemaphoreType.DMA((5, 9)),
+            pltpu.SemaphoreType.DMA((12, 9)),
+            pltpu.SemaphoreType.DMA((12, 9)),
         ],
         compiler_params=pltpu.CompilerParams(
             collective_id=0, has_side_effects=True
         ),
     )(fields, velocity, coupling, positions, log_radius, growth, rest_gap, gas_pressure,
       move_codes, targets)
-    return out, bub
+    here = functools.partial(pltpu.with_memory_space_constraint, memory_space=pltpu.VMEM)
+    return pl.pallas_call(
+        write_out,
+        out_shape=(
+            jax.ShapeDtypeStruct((nf, nz, ny, nx), f32),
+            jax.ShapeDtypeStruct((2, 1, 1, slots), f32),
+        ),
+        in_specs=[vmem, vmem],
+        out_specs=(pl.BlockSpec(memory_space=pl.ANY), pl.BlockSpec(memory_space=pl.ANY)),
+        scratch_shapes=[pltpu.SemaphoreType.DMA((ny + 1,))],
+    )(here(out), here(bub))
 
 
 def solution(mesh):

time: 29.2 us -> 25.4 us (0.87)
  Pallas kernels: 26.8 us -> 24.5 us
  local copies, waits for them, and re-layouts: 1.48 us -> 0 us
    pallas_call x1, Pallas kernels: 26.8 us -> 23.5 us  [shards(): pl.pallas_call(functools.partial(kernel, n_gx, n_gy, (nf, nz, ny, nx, slo...]
    unnamed x2 -> x0, local copies, waits for them, and re-layouts: 1.48 us -> none
    pallas_call x0 -> x1, Pallas kernels: none -> 1.01 us  [shards(): pl.pallas_call(write_out, out_shape=(jax.ShapeDtypeStruct((nf, nz, ny, nx...]
where the time goes in v3:
time: 25.4 us; the launch traced here: 25.2 us
  Pallas kernels  24.5 us (96%)
  between operations  0.64 us (3%)
    pallas_call x1, Pallas kernels, shards(): pl.pallas_call(functools.partial(kernel, n_gx, n_gy, (nf, nz, ny, nx, slo...  23.5 us
    pallas_call x1, Pallas kernels, shards(): pl.pallas_call(write_out, out_shape=(jax.ShapeDtypeStruct((nf, nz, ny, nx...  1.01 us

profile of v3, /device:TPU:1, one launch (start us, length us, event | category | flops | bytes accessed | tf_op | source)
XLA Modules:
  0.0 25.2 jit_solution(11753501342610621688)
XLA Ops:
  0.6 23.5 %shard_map.113 = (f32[6,16,16,128]{3,2,1,0:T(8,128)S(1)}, f32[2,1,1,1024]{3,2,1,0:T(1,128)S(1)}) custom-call(f32[6,16,16,128]{3,2,1,0:T(8,128)} %fields_ref.1, f32[2,16,16,128]{3,2,1,0:T(8,128)} %vel_ref.1, f32[6]{0:T(128)} %coup_hbm.1, f32[3,1,1,1024]{3,2,1,0:T(1,128)} %pos_hbm.1, f32[1,1,1024]{2,1,0:T(1,128)} %lr_hbm.1, f32[1,1,1024]{2,1,0:T(1,128)} %gr_hbm.1, ...), custom_call_target="tpu_custom_call" | custom-call | tf_op jit(solution)/shard_map/pallas_call | solution.py:672
  24.1 1.0 %shard_map.114 = (f32[6,16,16,128]{3,2,1,0:T(8,128)}, f32[2,1,1,1024]{3,2,1,0:T(1,128)}) custom-call(f32[6,16,16,128]{3,2,1,0:T(8,128)S(1)} %get-tuple-element.4.fields_ref, f32[2,1,1,1024]{3,2,1,0:T(1,128)S(1)} %get-tuple-element.5.bubbles_ref), custom_call_target="tpu_custom_call" | custom-call | tf_op jit(solution)/shard_map/pallas_call | solution.py:733

commit v4 on v3

--- a/solution.py
+++ b/solution.py
@@ -26,8 +26,9 @@
     t3 = d4 - d3
     x = 0.75 * d2
     y = 0.75 * d3
-    b0 = t1 * (t1 + x) + (x * d2 + smooth_eps)
-    b1 = t2 * t2 + (x * d3 + smooth_eps)
+    near = x * d2 + smooth_eps
+    b0 = t1 * (t1 + x) + near
+    b1 = t2 * (t2 + x) + near
     b2 = t3 * (t3 - y) + (y * d3 + smooth_eps)
     j1 = b0 / b1
     j2 = b0 / b2
@@ -119,6 +120,7 @@
     outbox,
     inbox,
     vals,
+    home_s,
     samp,
     wx,
     wzy,
@@ -212,6 +214,22 @@
     y_speed = list(y_msgs(q, nf, 1))
     smears = [list(smear_msgs(0)), list(smear_msgs(1))]
 
+    barrier = pltpu.get_barrier_semaphore()
+    neighbours = jnp.int32(0)
+    for c in DIRS:
+        ok = inside(c, 1)
+
+        @pl.when(ok)
+        def _():
+            pl.semaphore_signal(
+                barrier,
+                inc=1,
+                device_id=(me_x + (c // 3 - 1), me_y + (c % 3 - 1)),
+                device_id_type=pl.DeviceIdType.MESH,
+            )
+
+        neighbours = neighbours + ok.astype(jnp.int32)
+
     small = [
         pltpu.make_async_copy(src, dst, small_sem.at[n])
         for n, (src, dst) in enumerate(
@@ -244,22 +262,6 @@
         )
     for copy in loads:
         copy.start()
-
-    barrier = pltpu.get_barrier_semaphore()
-    neighbours = jnp.int32(0)
-    for c in DIRS:
-        ok = inside(c, 1)
-
-        @pl.when(ok)
-        def _():
-            pl.semaphore_signal(
-                barrier,
-                inc=1,
-                device_id=(me_x + (c // 3 - 1), me_y + (c % 3 - 1)),
-                device_id_type=pl.DeviceIdType.MESH,
-            )
-
-        neighbours = neighbours + ok.astype(jnp.int32)
 
     for copy in small:
         copy.wait()
@@ -352,7 +354,7 @@
     def halves(h):
         return pl.ds(pl.multiple_of(h * 8, 8), 8)
 
-    def inner_columns(buf, buft, first, stop):
+    def inner_columns(buf, buft):
         def body(k, carry):
             for j in range(lanes_at_once):
                 n = k * lanes_at_once + j
@@ -363,7 +365,7 @@
                 face_rows(buf, 3, ny - 5, f, halves(h))
             return carry
 
-        lax.fori_loop(first, stop, body, 0)
+        lax.fori_loop(0, nf * half // lanes_at_once, body, 0)
 
     def outer_column(buf, buft, f, h, slot):
         work = (dq_s.at[slot], df_s.at[slot], pair_s.at[slot])
@@ -383,10 +385,10 @@
             if p:
                 for c, src, dst in y_rims[p]:
                     recv(kind + p, c, src, dst)
+            for n in range(p * tiles // pieces, (p + 1) * tiles // pieces):
+                sums.append(sample_tile(n))
             for n in range(p * group_of * half, (p + 1) * group_of * half):
                 outer_column(buf, buft, n // half, n % half, n % 4)
-            for n in range(p * tiles // pieces, (p + 1) * tiles // pieces):
-                sums.append(sample_tile(n))
         return jnp.concatenate(sums, axis=1)
 
     def turn(value):
@@ -420,7 +422,6 @@
     pack_rims(qt, nf + 1, pk)
     y_tops(3, ny - 5)
     x_tops(range(1, last - 1))
-    inner_columns(q, qt, 0, 1)
 
     pl.semaphore_wait(barrier, neighbours)
     for c, src, dst in bubble_msgs:
@@ -435,24 +436,26 @@
         for c, src, dst in y_rims0[p]:
             send(5 + p, c, src, dst)
 
-    inner_columns(q, qt, 1, nf * half // lanes_at_once)
-
+    inner_columns(q, qt)
+
+    def homes_of(values):
+        slot = values[7:8].astype(jnp.int32) - 1
+        slot_hi = slot >> 7
+        slot_lo = slot & 127
+        total = values.shape[1]
+        place = jnp.where(
+            lax.broadcasted_iota(jnp.int32, (128, total), 0) == slot_lo, 1.0, 0.0
+        ).astype(jnp.bfloat16)
+        parts = split3_rows(values)
+        spread = jnp.concatenate(
+            [jnp.where(slot_hi == h, parts, 0.0) for h in range(chunks)], axis=0
+        )
+        return dot(spread.astype(jnp.bfloat16), place, True)
+
+    home_s[...] = homes_of(jnp.where(code == 4, vals[...], 0.0))
     for c, src, dst in bubble_msgs:
         recv(0, c, src, dst)
-    stay = jnp.where(code == 4, vals[...], 0.0)
-    all_vals = jnp.concatenate([stay] + [inbox[n] for n in range(8)], axis=1)
-    slot = all_vals[7:8].astype(jnp.int32) - 1
-    slot_hi = slot >> 7
-    slot_lo = slot & 127
-    total = all_vals.shape[1]
-    place = jnp.where(
-        lax.broadcasted_iota(jnp.int32, (128, total), 0) == slot_lo, 1.0, 0.0
-    ).astype(jnp.bfloat16)
-    all_parts = split3_rows(all_vals)
-    spread = jnp.concatenate(
-        [jnp.where(slot_hi == h, all_parts, 0.0) for h in range(chunks)], axis=0
-    )
-    homes = dot(spread.astype(jnp.bfloat16), place, True)
+    homes = home_s[...] + homes_of(jnp.concatenate([inbox[n] for n in range(8)], axis=1))
     bubbles = jnp.concatenate(
         [
             (homes[24 * h : 24 * h + 8] + homes[24 * h + 8 : 24 * h + 16])
@@ -499,16 +502,20 @@
             part = part + prod[8 * k : 8 * (k + 1)]
         return jnp.sum(part, axis=0, keepdims=True)
 
-    def deposit(s, volume):
+    def load_parts(volume):
         for k in range(4):
             at = pl.ds(k * step_rows, step_rows)
             hi, lo = split2(wzy[at] * volume)
             part_s[at] = hi
             part_s[pl.ds(rows + k * step_rows, step_rows)] = lo
-        both = dot(part_s[...], wx[pl.ds(0, width)], True)
-        d = (both[:rows] + both[rows:]) + dot(
-            part_s[pl.ds(0, rows)], wx[pl.ds(2 * width, width)], True
-        )
+
+    def deposit_product(at):
+        both = dot(part_s[:, at], wx[pl.ds(0, width), at], True)
+        return (both[:rows] + both[rows:]) + dot(
+            part_s[pl.ds(0, rows), at], wx[pl.ds(2 * width, width), at], True
+        )
+
+    def send_smear(s, d):
         rims = []
         for r in range(ny + 4):
             dep[s, r] = d[r * nz : (r + 1) * nz, :nx]
@@ -578,7 +585,8 @@
         return occupied * four_pi * jnp.exp(3.0 * s) * w
 
     s_zero, w_zero = bubbles[3:4], bubbles[4:5]
-    deposit(0, volume_of(s_zero, w_zero))
+    load_parts(volume_of(s_zero, w_zero))
+    send_smear(0, deposit_product(pl.ds(0, slots)))
 
     for c, src, dst in y_speed:
         recv(8, c, src, dst)
@@ -594,7 +602,8 @@
     sampled = outer_columns(q, qt, y_rims0, 5)
     s_one = s_zero + time_step * w_zero
     w_one = w_zero + time_step * rate_of(s_zero, w_zero, sampled)
-    deposit(1, volume_of(s_one, w_one))
+    load_parts(volume_of(s_one, w_one))
+    send_smear(1, deposit_product(pl.ds(0, slots)))
 
     merged = gather_smear(0)
 
@@ -619,7 +628,7 @@
     for c, src, dst in rims1:
         send(4, c, src, dst)
 
-    inner_columns(q1, qt1, 0, nf * half // lanes_at_once)
+    inner_columns(q1, qt1)
     for c, src, dst in rims1:
         recv(4, c, src, dst)
     for c, src, dst in y_rims1[0]:
@@ -709,6 +718,7 @@
             sc(8, 8, 128),
             sc(8, 8, 128),
             sc(8, slots),
+            sc(24 * (slots // 128), 128),
             pltpu.VMEM((rows, 6 * nx), jnp.bfloat16),
             pltpu.VMEM((6 * nx, slots), jnp.bfloat16),
             sc(rows, slots),

time: 25.4 us -> 25.3 us (level)
  no operation moved by 1% of the time
where the time goes in v4:
time: 25.3 us; the launch traced here: 25 us
  Pallas kernels  24.4 us (96%)
  between operations  0.64 us (3%)
    pallas_call x1, Pallas kernels, shards(): pl.pallas_call(functools.partial(kernel, n_gx, n_gy, (nf, nz, ny, nx, slo...  23.4 us
    pallas_call x1, Pallas kernels, shards(): pl.pallas_call(write_out, out_shape=(jax.ShapeDtypeStruct((nf, nz, ny, nx...  1.01 us

profile of v4, /device:TPU:1, one launch (start us, length us, event | category | flops | bytes accessed | tf_op | source)
XLA Modules:
  0.0 25.0 jit_solution(12506089696294153030)
XLA Ops:
  0.6 23.4 %shard_map.113 = (f32[6,16,16,128]{3,2,1,0:T(8,128)S(1)}, f32[2,1,1,1024]{3,2,1,0:T(1,128)S(1)}) custom-call(f32[6,16,16,128]{3,2,1,0:T(8,128)} %fields_ref.1, f32[2,16,16,128]{3,2,1,0:T(8,128)} %vel_ref.1, f32[6]{0:T(128)} %coup_hbm.1, f32[3,1,1,1024]{3,2,1,0:T(1,128)} %pos_hbm.1, f32[1,1,1024]{2,1,0:T(1,128)} %lr_hbm.1, f32[1,1,1024]{2,1,0:T(1,128)} %gr_hbm.1, ...), custom_call_target="tpu_custom_call" | custom-call | tf_op jit(solution)/shard_map/pallas_call | solution.py:681
  24.0 1.0 %shard_map.114 = (f32[6,16,16,128]{3,2,1,0:T(8,128)}, f32[2,1,1,1024]{3,2,1,0:T(1,128)}) custom-call(f32[6,16,16,128]{3,2,1,0:T(8,128)S(1)} %get-tuple-element.4.fields_ref, f32[2,1,1,1024]{3,2,1,0:T(1,128)S(1)} %get-tuple-element.5.bubbles_ref), custom_call_target="tpu_custom_call" | custom-call | tf_op jit(solution)/shard_map/pallas_call | solution.py:743

commit v5 on v4

--- a/solution.py
+++ b/solution.py
@@ -376,15 +376,20 @@
         ]
         turned = jnp.concatenate(blocks, axis=0).T
         dv[f, pl.ds(h * band, band)] = turned.reshape(band, nz, nx)
-        face_rows(buf, 0, 3, f, halves(h))
-        face_rows(buf, ny - 2, 3, f, halves(h))
-
-    def outer_columns(buf, buft, y_rims, kind):
+
+    def outer_rows(buf, y_rims, kind, p):
+        if p:
+            for c, src, dst in y_rims[p]:
+                recv(kind + p, c, src, dst)
+        for n in range(p * group_of * half, (p + 1) * group_of * half):
+            face_rows(buf, 0, 3, n // half, halves(n % half))
+            face_rows(buf, ny - 2, 3, n // half, halves(n % half))
+
+    def outer_columns(buf, buft, y_rims, kind, rows_too):
         sums = []
         for p in range(pieces):
-            if p:
-                for c, src, dst in y_rims[p]:
-                    recv(kind + p, c, src, dst)
+            if rows_too:
+                outer_rows(buf, y_rims, kind, p)
             for n in range(p * tiles // pieces, (p + 1) * tiles // pieces):
                 sums.append(sample_tile(n))
             for n in range(p * group_of * half, (p + 1) * group_of * half):
@@ -599,7 +604,7 @@
     y_tops(0, 3)
     y_tops(ny - 2, 3)
     x_tops((0, last - 1, last))
-    sampled = outer_columns(q, qt, y_rims0, 5)
+    sampled = outer_columns(q, qt, y_rims0, 5, True)
     s_one = s_zero + time_step * w_zero
     w_one = w_zero + time_step * rate_of(s_zero, w_zero, sampled)
     load_parts(volume_of(s_one, w_one))
@@ -629,13 +634,15 @@
         send(4, c, src, dst)
 
     inner_columns(q1, qt1)
+    for c, src, dst in y_rims1[0]:
+        recv(9, c, src, dst)
+    for p in range(pieces):
+        outer_rows(q1, y_rims1, 9, p)
     for c, src, dst in rims1:
         recv(4, c, src, dst)
-    for c, src, dst in y_rims1[0]:
-        recv(9, c, src, dst)
     unpack_rims(qt1, nf, pk1_in)
     fill_sample(q1, qt1, c1_in)
-    rate_two = rate_of(s_one, w_one, outer_columns(q1, qt1, y_rims1, 9))
+    rate_two = rate_of(s_one, w_one, outer_columns(q1, qt1, y_rims1, 9, False))
     s_two = 0.5 * s_zero + 0.5 * (s_one + time_step * w_one)
     w_two = 0.5 * w_zero + 0.5 * (w_one + time_step * rate_two)
     bub_ref[0, 0] = s_two * occupied

time: 25.3 us -> 24.5 us (0.968)
  Pallas kernels: 24.4 us -> 23.7 us
    pallas_call x1, Pallas kernels: 23.4 us -> 22.7 us  [shards(): pl.pallas_call(functools.partial(kernel, n_gx, n_gy, (nf, nz, ny, nx, slo...]
where the time goes in v5:
time: 24.5 us; the launch traced here: 24.3 us
  Pallas kernels  23.7 us (97%)
  between operations  0.64 us (3%)
    pallas_call x1, Pallas kernels, shards(): pl.pallas_call(functools.partial(kernel, n_gx, n_gy, (nf, nz, ny, nx, slo...  22.7 us
    pallas_call x1, Pallas kernels, shards(): pl.pallas_call(write_out, out_shape=(jax.ShapeDtypeStruct((nf, nz, ny, nx...  1.01 us

profile of v5, /device:TPU:1, one launch (start us, length us, event | category | flops | bytes accessed | tf_op | source)
XLA Modules:
  0.0 24.3 jit_solution(24307612168928562)
XLA Ops:
  0.6 22.7 %shard_map.113 = (f32[6,16,16,128]{3,2,1,0:T(8,128)S(1)}, f32[2,1,1,1024]{3,2,1,0:T(1,128)S(1)}) custom-call(f32[6,16,16,128]{3,2,1,0:T(8,128)} %fields_ref.1, f32[2,16,16,128]{3,2,1,0:T(8,128)} %vel_ref.1, f32[6]{0:T(128)} %coup_hbm.1, f32[3,1,1,1024]{3,2,1,0:T(1,128)} %pos_hbm.1, f32[1,1,1024]{2,1,0:T(1,128)} %lr_hbm.1, f32[1,1,1024]{2,1,0:T(1,128)} %gr_hbm.1, ...), custom_call_target="tpu_custom_call" | custom-call | tf_op jit(solution)/shard_map/pallas_call | solution.py:688
  23.3 1.0 %shard_map.114 = (f32[6,16,16,128]{3,2,1,0:T(8,128)}, f32[2,1,1,1024]{3,2,1,0:T(1,128)}) custom-call(f32[6,16,16,128]{3,2,1,0:T(8,128)S(1)} %get-tuple-element.4.fields_ref, f32[2,1,1,1024]{3,2,1,0:T(1,128)S(1)} %get-tuple-element.5.bubbles_ref), custom_call_target="tpu_custom_call" | custom-call | tf_op jit(solution)/shard_map/pallas_call | solution.py:750
